TPU v7x, 32 devices: a whole 2x2x4 slice. The times are simulated.
32 devices in a mesh: tok: 8 (over z, x), col: 4 (over y, core).
Axes of the slice: x: 2, y: 2, z: 4, core: 2. Of those that a mesh axis runs over, the one named last changes fastest.
Arguments:
- tokens: bfloat16 [2560, 4096], P('tok', 'col'), may hold values from -16 to 16
- w_query: bfloat16 [4096, 2048], P(None, 'col'), may hold values from -0.09375 to 0.09375
- w_key: bfloat16 [4096, 512], P(None, 'col'), may hold values from -0.09375 to 0.09375
- w_value: bfloat16 [4096, 512], P(None, 'col'), may hold values from -0.09375 to 0.09375
- w_out: bfloat16 [2048, 4096], P('col'), may hold values from -0.125 to 0.125
- block_ids: int32 [16, 40, 16], P('col', 'tok'), may hold values from 0 to 39, as said below
- block_counts: int32 [16, 40], P('col', 'tok'), may hold values from 1 to 16, as said below
Outputs:
- mixed: bfloat16 [2560, 4096], P('tok', 'col')
Inputs may be any that keep to these rules, and one draw needn't show every extreme that they name: block_ids[h, b, 0] = b; the slots below block_counts[h, b] hold distinct blocks none after b; later slots hold block numbers that are not read. block_counts[h, b] <= b + 1; densities differ from head to head, and some row of some head uses all 16 slots.
All inputs are finite; a program needn't handle non-finite values.
Results may differ from a plain program's by a relative error of at most 0.012.
Values may be sent and summed in bfloat16 or wider, within the bound.
No kernel may reach another device: no remote copies, remote signals or barrier semaphores. Data moves between devices by JAX's collectives and lax.ppermute only.
A program may use at most 64 MiB of HBM per device.

v0:
```python
import functools

import jax
import jax.numpy as jnp
from jax import lax
from jax.experimental import pallas as pl
from jax.experimental.pallas import tpu as pltpu
from jax.sharding import PartitionSpec as P


HEAD_SIZE = 128
BLK = 64
GROUP_BLOCKS = 4
ROPE_BASE = 500000.0
NEG = -1e30


SMEM = pl.BlockSpec(memory_space=pltpu.SMEM)
VMEM = pl.BlockSpec(memory_space=pltpu.VMEM)
HBM = pl.BlockSpec(memory_space=pltpu.HBM)

bf16, f32 = jnp.bfloat16, jnp.float32


def shape(dims, kind=bf16):
    return jax.ShapeDtypeStruct(dims, kind)


def call(kernel, ins, outs, args, flops, scratch=(), vmem=10, grown=0):
    args = [
        pltpu.with_memory_space_constraint(arg, pltpu.HBM) if spec is HBM else arg
        for spec, arg in zip(ins, args)
    ]
    moved = sum(x.size * x.dtype.itemsize for x in jax.tree.leaves((outs, args)))
    return pl.pallas_call(
        kernel,
        out_shape=outs,
        in_specs=ins,
        out_specs=jax.tree.map(lambda _: VMEM, outs),
        scratch_shapes=list(scratch),
        compiler_params=pltpu.CompilerParams(vmem_limit_bytes=vmem << 20),
        cost_estimate=pl.CostEstimate(
            flops=flops, transcendentals=grown, bytes_accessed=moved
        ),
    )(*args)


def dot(a, b):
    return jnp.dot(a, b, preferred_element_type=f32)


def turn_tables(positions):
    half = HEAD_SIZE // 2
    freq = ROPE_BASE ** (-jnp.arange(half, dtype=f32) / half)
    angle = positions[:, None] * freq[None, :]
    cosine, sine = jnp.cos(angle), jnp.sin(angle)
    return (
        jnp.concatenate([cosine, cosine], axis=1),
        jnp.concatenate([-sine, sine], axis=1),
    )


def run_copies(pairs, sem):
    copies = [
        pltpu.make_async_copy(source, target, sem.at[index])
        for index, (source, target) in enumerate(pairs)
    ]
    for copy in copies:
        copy.start()
    for copy in copies:
        copy.wait()


def split_kernel(spans, tokens, *rest):
    outs, sem = rest[:-1], rest[-1]
    run_copies(
        [(tokens.at[pl.ds(a, b - a)], out) for (a, b), out in zip(spans, outs)], sem
    )


def columns_kernel(starts_ref, wo, *rest):
    outs, sem = rest[:-1], rest[-1]
    feat = outs[0].shape[1]
    run_copies(
        [
            (wo.at[:, pl.ds(pl.multiple_of(starts_ref[index], feat), feat)], out)
            for index, out in enumerate(outs)
        ],
        sem,
    )


def rows_kernel(starts_ref, *rest):
    sources, outs, sem = rest[:3], rest[3:-1], rest[-1]
    feat = outs[0].shape[0]
    pairs = []
    for index, out in enumerate(outs):
        rows = pl.ds(pl.multiple_of(starts_ref[index], feat), feat)
        at = 0
        for source in sources:
            width = source.shape[1]
            pairs.append((source.at[rows, :], out.at[:, pl.ds(at, width)]))
            at += width
    run_copies(pairs, sem)


def near_kernel(spans, own_ref, near_ref, w0, w1, *outs):
    for (a, b), out in zip(spans, outs):
        out[...] = dot(own_ref[a:b], w0[...]) + dot(near_ref[a:b], w1[...])


def far_kernel(far_ref, sum_ref, w, out_ref):
    out_ref[...] = sum_ref[...] + dot(far_ref[...], w[...])


def last_kernel(a, b, far_ref, sum_ref, cos_ref, sin_ref, w, q_ref, kv_ref):
    product = sum_ref[...] + dot(far_ref[...], w[...])
    cosine, sine = cos_ref[a:b], sin_ref[a:b]
    width = q_ref.shape[1]
    for at in range(0, width + HEAD_SIZE, HEAD_SIZE):
        piece = product[:, at : at + HEAD_SIZE]
        turned = piece * cosine + pltpu.roll(piece, HEAD_SIZE // 2, 1) * sine
        if at < width:
            q_ref[:, at : at + HEAD_SIZE] = turned.astype(bf16)
        else:
            kv_ref[:, :HEAD_SIZE] = turned.astype(bf16)
    kv_ref[:, HEAD_SIZE:] = product[:, width + HEAD_SIZE :].astype(bf16)


def out_kernel(own_ref, partner_ref, own_w, partner_w, out_ref):
    total = dot(own_ref[...], own_w[...]) + dot(partner_ref[...], partner_w[...])
    out_ref[...] = total.astype(out_ref.dtype)


def final_kernel(spans, *refs):
    out_ref = refs[-1]
    count = len(spans)
    for (a, b), kept, arrived in zip(spans, refs[:count], refs[count : 2 * count]):
        out_ref[a:b] = (kept[...] + arrived[...].astype(f32)).astype(bf16)


def attend_kernel(heads, qblocks, nsel, count, *refs):
    offsets_ref, counts_ref, q_ref = refs[:3]
    parts = refs[3 : 3 + count]
    out_ref, kv_ref = refs[3 + count :]
    at = 0
    for part in parts:
        kv_ref[at : at + part.shape[0]] = part[...]
        at += part.shape[0]
    width = GROUP_BLOCKS * BLK
    groups = nsel // GROUP_BLOCKS
    scale = HEAD_SIZE**-0.5

    def one_qblock(qb, carry):
        lane = lax.broadcasted_iota(jnp.int32, (BLK, width), 1)
        row = lax.broadcasted_iota(jnp.int32, (BLK, width), 0)
        rows = pl.ds(pl.multiple_of(qb * BLK, BLK), BLK)
        for head in range(heads):
            columns = slice(head * HEAD_SIZE, (head + 1) * HEAD_SIZE)
            query = q_ref[rows, columns]
            place = head * qblocks[2] + qblocks[0] + qb
            live = counts_ref[place]
            scores = []
            values = []
            for group in range(groups):
                pieces = []
                for slot in range(GROUP_BLOCKS):
                    start = offsets_ref[place * nsel + group * GROUP_BLOCKS + slot]
                    pieces.append(kv_ref[pl.ds(pl.multiple_of(start, BLK), BLK), :])
                both = jnp.concatenate(pieces, axis=0)
                values.append(both[:, HEAD_SIZE:])
                score = lax.dot_general(
                    query,
                    both[:, :HEAD_SIZE],
                    (((1,), (1,)), ((), ())),
                    preferred_element_type=f32,
                )
                allowed = lane < (live - group * GROUP_BLOCKS) * BLK
                if group == 0:
                    allowed = allowed & ((lane >= BLK) | (lane <= row))
                scores.append(jnp.where(allowed, score, NEG))
            highest = jnp.max(
                functools.reduce(jnp.maximum, scores), axis=-1, keepdims=True
            )
            total = jnp.zeros((BLK, width), f32)
            summed = jnp.zeros((BLK, HEAD_SIZE), f32)
            for score, value in zip(scores, values):
                weights = jnp.exp((score - highest) * scale)
                total = total + weights
                summed = summed + dot(weights.astype(bf16), value)
            total = jnp.sum(total, axis=-1, keepdims=True)
            out_ref[rows, columns] = (summed / total).astype(bf16)
        return carry

    lax.fori_loop(0, qblocks[1] - qblocks[0], one_qblock, 0)


def attend(offsets, counts, query, parts, heads, qblocks, nsel):
    pairs = query.size // HEAD_SIZE * nsel * BLK
    held = sum(part.size for part in parts) * 2 >> 20
    return call(
        functools.partial(attend_kernel, heads, qblocks, nsel, len(parts)),
        [SMEM, SMEM, VMEM] + [VMEM] * len(parts),
        shape(query.shape),
        (offsets, counts, query, *parts),
        4 * pairs * HEAD_SIZE,
        scratch=[pltpu.VMEM((sum(p.shape[0] for p in parts), 2 * HEAD_SIZE), bf16)],
        vmem=8 + 3 * held,
        grown=pairs,
    )


def on_device(mesh, tokens, w_query, w_key, w_value, w_out, block_ids, block_counts):
    cols, toks = mesh.shape["col"], mesh.shape["tok"]
    tok_rows, feat = tokens.shape
    heads = w_query.shape[1] // HEAD_SIZE
    qblocks, nsel = block_ids.shape[1:]
    col = lax.axis_index("col")
    tok = lax.axis_index("tok")
    lines = toks // 2
    inner = w_out.shape[0]
    ws = (w_query, w_key, w_value)
    width = sum(w.shape[1] for w in ws)

    def over_col(value, flip):
        return lax.ppermute(value, "col", [(i, i ^ flip) for i in range(cols)])

    def across(value):
        return lax.ppermute(value, "tok", [(i, i ^ 1) for i in range(toks)])

    def up(value, steps):
        return lax.ppermute(
            value, "tok", [(i, (i + 2 * steps) % toks) for i in range(toks)]
        )

    first = (qblocks + 1) // 2 * BLK
    spans = [(0, first), (first, tok_rows)]
    starts = (col ^ jnp.arange(4, dtype=jnp.int32)) * feat
    pieces = call(
        functools.partial(split_kernel, spans),
        [HBM],
        [shape((b - a, feat)) for a, b in spans],
        (tokens,),
        0,
        scratch=[pltpu.SemaphoreType.DMA((len(spans),))],
    )
    far_parts = []
    for piece in pieces:
        far_parts.append(over_col(piece, 2))
    near = over_col(tokens, 1)
    block_ids, block_counts, _ = lax.optimization_barrier(
        (block_ids, block_counts, pieces[0])
    )
    positions = (tok * tok_rows + jnp.arange(tok_rows, dtype=jnp.int32)).astype(f32)
    cosine, sine = turn_tables(positions)
    live = jnp.arange(nsel, dtype=jnp.int32)[None, None, :] < block_counts[:, :, None]
    owner, inside = block_ids // qblocks, block_ids % qblocks
    slot = (tok // 2 - owner // 2) * 2 + ((owner % 2) ^ (tok % 2))
    own = jnp.arange(qblocks, dtype=jnp.int32)[None, :, None] * BLK
    offsets = jnp.where(live, slot * tok_rows + inside * BLK, own).reshape(-1)
    counts = block_counts.reshape(-1)
    starts, cosine, sine, offsets, counts = lax.optimization_barrier(
        (starts, cosine, sine, offsets, counts)
    )
    out_own_near, out_send_near, out_own_far, out_send_far = call(
        columns_kernel,
        [SMEM, HBM],
        [shape((inner, feat))] * 4,
        (starts, w_out),
        0,
        scratch=[pltpu.SemaphoreType.DMA((4,))],
    )
    partner_near = over_col(out_send_near, 1)
    partner_far = over_col(out_send_far, 1)
    weights = call(
        rows_kernel,
        [SMEM, HBM, HBM, HBM],
        [shape((feat, width))] * 4,
        (starts, *ws),
        0,
        scratch=[pltpu.SemaphoreType.DMA((12,))],
    )
    sums = call(
        functools.partial(near_kernel, spans),
        [VMEM] * 4,
        [shape((b - a, width), f32) for a, b in spans],
        (tokens, near, weights[0], weights[1]),
        4 * tok_rows * feat * width,
    )

    queries = []
    shards = [[] for _ in range(toks)]
    for (a, b), far, summed in zip(spans, far_parts, sums):
        rows = b - a
        opposite = over_col(far, 1)
        summed = call(
            far_kernel,
            [VMEM] * 3,
            shape((rows, width), f32),
            (far, summed, weights[2]),
            2 * rows * feat * width,
        )
        query, pair = call(
            functools.partial(last_kernel, a, b),
            [VMEM] * 5,
            [shape((rows, heads * HEAD_SIZE)), shape((rows, 2 * HEAD_SIZE))],
            (opposite, summed, cosine, sine, weights[3]),
            2 * rows * feat * width,
        )
        queries.append(query)
        for line in range(lines):
            moved = pair
            if line:
                moved = up(pair, line)
            shards[2 * line + 1].append(across(moved))
            shards[2 * line].append(moved)
    parts = [piece for shard in shards for piece in shard]

    keeps, arrivals = [], []
    for (a, b), query in zip(spans, queries):
        rows, qa, qb = b - a, a // BLK, b // BLK
        attended = attend(offsets, counts, query, parts, heads, (qa, qb, qblocks), nsel)
        partner = over_col(attended, 1)

        def project(own_w, partner_w, kind):
            return call(
                out_kernel,
                [VMEM] * 4,
                shape((rows, feat), kind),
                (attended, partner, own_w, partner_w),
                4 * rows * feat * inner,
            )

        sent = project(out_own_far, partner_far, bf16)
        arrivals.append(over_col(sent, 2))
        keeps.append(project(out_own_near, partner_near, f32))
    return call(
        functools.partial(final_kernel, spans),
        [VMEM] * (2 * len(spans)),
        shape((tok_rows, feat)),
        (*keeps, *arrivals),
        tok_rows * feat,
    )


def solution(mesh):
    in_specs = (
        P("tok", "col"),
        P(None, "col"),
        P(None, "col"),
        P(None, "col"),
        P("col", None),
        P("col", "tok", None),
        P("col", "tok"),
    )

    def body(*args):
        return on_device(mesh, *args)

    return jax.shard_map(
        body,
        mesh=mesh,
        in_specs=in_specs,
        out_specs=P("tok", "col"),
        check_vma=False,
    )
```

profile of v0, /device:TPU:0, one launch (start us, length us, event | category | flops | bytes accessed | tf_op | source)
XLA Modules:
  0.0 85.5 jit_solution(4732749489020313852)
XLA Ops:
  0.5 1.1 %shard_map.73 = (bf16[192,1024]{1,0:T(8,128)(2,1)S(1)}, bf16[128,1024]{1,0:T(8,128)(2,1)S(1)}) custom-call(bf16[320,1024]{1,0:T(8,128)(2,1)} %own_ref.1), custom_call_target="tpu_custom_call" | custom-call | bytes 1310720 | tf_op jit(solution)/shard_map/pallas_call | solution.py:35
  1.6 2.6 %collective-permute-start.3 = (bf16[128,1024]{1,0:T(8,128)(2,1)S(1)}, bf16[128,1024]{1,0:T(8,128)(2,1)S(1)}, u32[]{:S(2)}, u32[]{:S(2)}) collective-permute-start(bf16[128,1024]{1,0:T(8,128)(2,1)S(1)} %get-tuple-element.43), channel_id=1, source_target_pairs={{0,2},{1,3},{2,0},{3,1},{4,6},{5,7},{6,4},{7,5},{8,10},{9,11},{10,... | collective-permute-start | bytes 786440 | tf_op jit(solution)/shard_map/ppermute | solution.py:226
  4.3 0.8 copy.9
  5.7 0.8 fusion.6
  6.5 0.8 reshape.24.refs_1_
  7.5 2.8 %shard_map.81 = (bf16[512,1024]{1,0:T(8,128)(2,1)S(1)}, bf16[512,1024]{1,0:T(8,128)(2,1)S(1)}, bf16[512,1024]{1,0:T(8,128)(2,1)S(1)}, bf16[512,1024]{1,0:T(8,128)(2,1)S(1)}) custom-call(s32[4]{0:T(128)S(1)} %xor_multiply_fusion.starts_ref, bf16[512,4096]{1,0:T(8,128)(2,1)} %wo.1), custom_call_target="tpu_custom_call" | custom-call | bytes 8388624 | tf_op jit(solution)/shard_map/pallas_call | solution.py:35
  10.6 9.0 %collective-permute-done.far_ref = bf16[192,1024]{1,0:T(8,128)(2,1)S(1)} collective-permute-done((bf16[192,1024]{1,0:T(8,128)(2,1)S(1)}, bf16[192,1024]{1,0:T(8,128)(2,1)S(1)}, u32[]{:S(2)}, u32[]{:S(2)}) %collective-permute-start) | collective-permute-done | bytes 393248 | tf_op jit(solution)/shard_map/ppermute | solution.py:226
  20.1 3.4 %shard_map.74 = (bf16[1024,768]{1,0:T(8,128)(2,1)S(1)}, bf16[1024,768]{1,0:T(8,128)(2,1)S(1)}, bf16[1024,768]{1,0:T(8,128)(2,1)S(1)}, bf16[1024,768]{1,0:T(8,128)(2,1)S(1)}) custom-call(s32[4]{0:T(128)S(1)} %xor_multiply_fusion.starts_ref, bf16[4096,512]{1,0:T(8,128)(2,1)} %rest_0_.1, bf16[4096,128]{1,0:T(8,128)(2,1)} %rest_1_.1, bf16[4096,128]{1,0:T(8,128)(2,1)} %rest_2_.1), custom_call_target="tpu_custom_call" | custom-call | bytes 12582928 | tf_op jit(solution)/shard_map/pallas_call | solution.py:35
  23.6 1.2 %shard_map.75 = (f32[192,768]{1,0:T(8,128)S(1)}, f32[128,768]{1,0:T(8,128)S(1)}) custom-call(bf16[320,1024]{1,0:T(8,128)(2,1)S(1)} %copy-done, bf16[320,1024]{1,0:T(8,128)(2,1)S(1)} %collective-permute-done.2.near_ref, bf16[1024,768]{1,0:T(8,128)(2,1)S(1)} %get-tuple-element.34.w0, bf16[1024,768]{1,0:T(8,128)(2,1)S(1)} %get-tuple-element.35.w1), custom_call_target="tpu_custom_call" | custom-call | flops 1006632960 | bytes 5439488 | tf_op jit(solution)/shard_map/pallas_call | solution.py:35
  25.7 1.8 %collective-permute-start.8 = (bf16[128,256]{1,0:T(8,128)(2,1)S(1)}, bf16[128,256]{1,0:T(8,128)(2,1)S(1)}, u32[]{:S(2)}, u32[]{:S(2)}) collective-permute-start(bf16[128,256]{1,0:T(8,128)(2,1)S(1)} %get-tuple-element.45.refs_4_), channel_id=1, source_target_pairs={{0,8},{4,12},{8,16},{12,20},{16,24},{20,28},{24,0},{28,4},{1,9},{5... | collective-permute-start | bytes 196616 | tf_op jit(solution)/shard_map/ppermute | solution.py:232
  27.5 2.6 %collective-permute-start.12 = (bf16[128,256]{1,0:T(8,128)(2,1)S(1)}, bf16[128,256]{1,0:T(8,128)(2,1)S(1)}, u32[]{:S(2)}, u32[]{:S(2)}) collective-permute-start(bf16[128,256]{1,0:T(8,128)(2,1)S(1)} %get-tuple-element.45.refs_4_), channel_id=1, source_target_pairs={{0,16},{4,20},{8,24},{12,28},{16,0},{20,4},{24,8},{28,12},{1,17},{... | collective-permute-start | bytes 196616 | tf_op jit(solution)/shard_map/ppermute | solution.py:232
  30.1 2.3 %collective-permute-done.8.refs_8_ = bf16[128,256]{1,0:T(8,128)(2,1)S(1)} collective-permute-done((bf16[128,256]{1,0:T(8,128)(2,1)S(1)}, bf16[128,256]{1,0:T(8,128)(2,1)S(1)}, u32[]{:S(2)}, u32[]{:S(2)}) %collective-permute-start.8) | collective-permute-done | bytes 65568 | tf_op jit(solution)/shard_map/ppermute | solution.py:232
  32.4 2.5 %collective-permute-start.16 = (bf16[128,256]{1,0:T(8,128)(2,1)S(1)}, bf16[128,256]{1,0:T(8,128)(2,1)S(1)}, u32[]{:S(2)}, u32[]{:S(2)}) collective-permute-start(bf16[128,256]{1,0:T(8,128)(2,1)S(1)} %get-tuple-element.45.refs_4_), channel_id=1, source_target_pairs={{0,24},{4,28},{8,0},{12,4},{16,8},{20,12},{24,16},{28,20},{1,25},{... | collective-permute-start | bytes 196616 | tf_op jit(solution)/shard_map/ppermute | solution.py:232
  35.1 1.5 %collective-permute-start.6 = (bf16[128,256]{1,0:T(8,128)(2,1)S(1)}, bf16[128,256]{1,0:T(8,128)(2,1)S(1)}, u32[]{:S(2)}, u32[]{:S(2)}) collective-permute-start(bf16[128,256]{1,0:T(8,128)(2,1)S(1)} %get-tuple-element.45.refs_4_), channel_id=1, source_target_pairs={{0,4},{4,0},{8,12},{12,8},{16,20},{20,16},{24,28},{28,24},{1,5},{5... | collective-permute-start | bytes 196616 | tf_op jit(solution)/shard_map/ppermute | solution.py:229
  38.5 1.4 %collective-permute-done.6.refs_6_ = bf16[128,256]{1,0:T(8,128)(2,1)S(1)} collective-permute-done((bf16[128,256]{1,0:T(8,128)(2,1)S(1)}, bf16[128,256]{1,0:T(8,128)(2,1)S(1)}, u32[]{:S(2)}, u32[]{:S(2)}) %collective-permute-start.6) | collective-permute-done | bytes 65568 | tf_op jit(solution)/shard_map/ppermute | solution.py:229
  39.9 1.4 %collective-permute-start.14 = (bf16[128,256]{1,0:T(8,128)(2,1)S(1)}, bf16[128,256]{1,0:T(8,128)(2,1)S(1)}, u32[]{:S(2)}, u32[]{:S(2)}) collective-permute-start(bf16[128,256]{1,0:T(8,128)(2,1)S(1)} %collective-permute-done.12.refs_12_), channel_id=1, source_target_pairs={{0,4},{4,0},{8,12},{12,8},{16,20},{20,16},{24,28},{28,24},{1,5},{5... | collective-permute-start | bytes 196616 | tf_op jit(solution)/shard_map/ppermute | solution.py:229
  42.0 2.1 %collective-permute-done.14.refs_14_ = bf16[128,256]{1,0:T(8,128)(2,1)S(1)} collective-permute-done((bf16[128,256]{1,0:T(8,128)(2,1)S(1)}, bf16[128,256]{1,0:T(8,128)(2,1)S(1)}, u32[]{:S(2)}, u32[]{:S(2)}) %collective-permute-start.14) | collective-permute-done | bytes 65568 | tf_op jit(solution)/shard_map/ppermute | solution.py:229
  44.1 1.8 %collective-permute-start.15 = (bf16[192,256]{1,0:T(8,128)(2,1)S(1)}, bf16[192,256]{1,0:T(8,128)(2,1)S(1)}, u32[]{:S(2)}, u32[]{:S(2)}) collective-permute-start(bf16[192,256]{1,0:T(8,128)(2,1)S(1)} %get-tuple-element.42.refs_3_), channel_id=1, source_target_pairs={{0,24},{4,28},{8,0},{12,4},{16,8},{20,12},{24,16},{28,20},{1,25},{... | collective-permute-start | bytes 294920 | tf_op jit(solution)/shard_map/ppermute | solution.py:232
  45.9 1.4 %collective-permute-start.7 = (bf16[192,256]{1,0:T(8,128)(2,1)S(1)}, bf16[192,256]{1,0:T(8,128)(2,1)S(1)}, u32[]{:S(2)}, u32[]{:S(2)}) collective-permute-start(bf16[192,256]{1,0:T(8,128)(2,1)S(1)} %get-tuple-element.42.refs_3_), channel_id=1, source_target_pairs={{0,8},{4,12},{8,16},{12,20},{16,24},{20,28},{24,0},{28,4},{1,9},{5... | collective-permute-start | bytes 294920 | tf_op jit(solution)/shard_map/ppermute | solution.py:232
  48.0 1.8 %collective-permute-done.15.refs_15_ = bf16[192,256]{1,0:T(8,128)(2,1)S(1)} collective-permute-done((bf16[192,256]{1,0:T(8,128)(2,1)S(1)}, bf16[192,256]{1,0:T(8,128)(2,1)S(1)}, u32[]{:S(2)}, u32[]{:S(2)}) %collective-permute-start.15) | collective-permute-done | bytes 98336 | tf_op jit(solution)/shard_map/ppermute | solution.py:232
  49.8 1.2 %collective-permute-start.13 = (bf16[192,256]{1,0:T(8,128)(2,1)S(1)}, bf16[192,256]{1,0:T(8,128)(2,1)S(1)}, u32[]{:S(2)}, u32[]{:S(2)}) collective-permute-start(bf16[192,256]{1,0:T(8,128)(2,1)S(1)} %collective-permute-done.11.refs_11_), channel_id=1, source_target_pairs={{0,4},{4,0},{8,12},{12,8},{16,20},{20,16},{24,28},{28,24},{1,5},{5... | collective-permute-start | bytes 294920 | tf_op jit(solution)/shard_map/ppermute | solution.py:229
  51.0 1.3 %collective-permute-done.7.refs_7_ = bf16[192,256]{1,0:T(8,128)(2,1)S(1)} collective-permute-done((bf16[192,256]{1,0:T(8,128)(2,1)S(1)}, bf16[192,256]{1,0:T(8,128)(2,1)S(1)}, u32[]{:S(2)}, u32[]{:S(2)}) %collective-permute-start.7) | collective-permute-done | bytes 98336 | tf_op jit(solution)/shard_map/ppermute | solution.py:232
  52.3 1.0 %collective-permute-start.17 = (bf16[192,256]{1,0:T(8,128)(2,1)S(1)}, bf16[192,256]{1,0:T(8,128)(2,1)S(1)}, u32[]{:S(2)}, u32[]{:S(2)}) collective-permute-start(bf16[192,256]{1,0:T(8,128)(2,1)S(1)} %collective-permute-done.15.refs_15_), channel_id=1, source_target_pairs={{0,4},{4,0},{8,12},{12,8},{16,20},{20,16},{24,28},{28,24},{1,5},{5... | collective-permute-start | bytes 294920 | tf_op jit(solution)/shard_map/ppermute | solution.py:229
  53.3 1.0 %collective-permute-start.9 = (bf16[192,256]{1,0:T(8,128)(2,1)S(1)}, bf16[192,256]{1,0:T(8,128)(2,1)S(1)}, u32[]{:S(2)}, u32[]{:S(2)}) collective-permute-start(bf16[192,256]{1,0:T(8,128)(2,1)S(1)} %collective-permute-done.7.refs_7_), channel_id=1, source_target_pairs={{0,4},{4,0},{8,12},{12,8},{16,20},{20,16},{24,28},{28,24},{1,5},{5... | collective-permute-start | bytes 294920 | tf_op jit(solution)/shard_map/ppermute | solution.py:229
  54.4 0.7 collective-permute-done.13.refs_13_
  55.1 1.9 %collective-permute-done.17.refs_17_ = bf16[192,256]{1,0:T(8,128)(2,1)S(1)} collective-permute-done((bf16[192,256]{1,0:T(8,128)(2,1)S(1)}, bf16[192,256]{1,0:T(8,128)(2,1)S(1)}, u32[]{:S(2)}, u32[]{:S(2)}) %collective-permute-start.17) | collective-permute-done | bytes 98336 | tf_op jit(solution)/shard_map/ppermute | solution.py:229
  57.0 1.1 %collective-permute-done.9.refs_9_ = bf16[192,256]{1,0:T(8,128)(2,1)S(1)} collective-permute-done((bf16[192,256]{1,0:T(8,128)(2,1)S(1)}, bf16[192,256]{1,0:T(8,128)(2,1)S(1)}, u32[]{:S(2)}, u32[]{:S(2)}) %collective-permute-start.9) | collective-permute-done | bytes 98336 | tf_op jit(solution)/shard_map/ppermute | solution.py:229
  58.0 5.0 %shard_map.80.own_ref = bf16[192,512]{1,0:T(8,128)(2,1)S(1)} custom-call(s32[320]{0:T(512)S(1)} %reshape.23.refs_0_, s32[20]{0:T(128)S(1)} %reshape.24.refs_1_, bf16[192,512]{1,0:T(8,128)(2,1)S(1)} %get-tuple-element.41.refs_2_, bf16[192,256]{1,0:T(8,128)(2,1)S(1)} %get-tuple-element.42.refs_3_, bf16[128,256]{1,0:T(8,128)(2,1)S(1)} %get-tuple-element.45.refs_4_, ...), custom_call_target="tpu_custom_call" | custom-call | flops 402653184 | bytes 1705296 | tf_op jit(solution)/shard_map/pallas_call | solution.py:35
  63.1 3.6 %shard_map.83.own_ref = bf16[128,512]{1,0:T(8,128)(2,1)S(1)} custom-call(s32[320]{0:T(512)S(1)} %reshape.23.refs_0_, s32[20]{0:T(128)S(1)} %reshape.24.refs_1_, bf16[128,512]{1,0:T(8,128)(2,1)S(1)} %get-tuple-element.48.refs_2_, bf16[192,256]{1,0:T(8,128)(2,1)S(1)} %get-tuple-element.42.refs_3_, bf16[128,256]{1,0:T(8,128)(2,1)S(1)} %get-tuple-element.45.refs_4_, ...), custom_call_target="tpu_custom_call" | custom-call | flops 268435456 | bytes 1574224 | tf_op jit(solution)/shard_map/pallas_call | solution.py:35
  67.8 1.6 %collective-permute-start.23 = (bf16[192,1024]{1,0:T(8,128)(2,1)S(1)}, bf16[192,1024]{1,0:T(8,128)(2,1)S(1)}, u32[]{:S(2)}, u32[]{:S(2)}) collective-permute-start(bf16[192,1024]{1,0:T(8,128)(2,1)S(1)} %shard_map.85), channel_id=1, source_target_pairs={{0,2},{1,3},{2,0},{3,1},{4,6},{5,7},{6,4},{7,5},{8,10},{9,11},{10,... | collective-permute-start | bytes 1179656 | tf_op jit(solution)/shard_map/ppermute | solution.py:226
  71.5 13.0 %collective-permute-done.24.refs_3_ = bf16[128,1024]{1,0:T(8,128)(2,1)S(1)} collective-permute-done((bf16[128,1024]{1,0:T(8,128)(2,1)S(1)}, bf16[128,1024]{1,0:T(8,128)(2,1)S(1)}, u32[]{:S(2)}, u32[]{:S(2)}) %collective-permute-start.24) | collective-permute-done | bytes 262176 | tf_op jit(solution)/shard_map/ppermute | solution.py:226
  84.6 0.9 %shard_map.87 = bf16[320,1024]{1,0:T(8,128)(2,1)} custom-call(f32[192,1024]{1,0:T(8,128)S(1)} %shard_map.82.refs_0_, f32[128,1024]{1,0:T(8,128)S(1)} %shard_map.84.refs_1_, bf16[192,1024]{1,0:T(8,128)(2,1)S(1)} %collective-permute-done.23.refs_2_, bf16[128,1024]{1,0:T(8,128)(2,1)S(1)} %collective-permute-done.24.refs_3_), custom_call_target="tpu_custom_call" | custom-call | flops 327680 | bytes 2621440 | tf_op jit(solution)/shard_map/pallas_call | solution.py:35
  (46 shorter events, 10.0 us)
Async XLA Ops:
  0.0 23.6 %collective-permute-start.2 = (bf16[320,1024]{1,0:T(8,128)(2,1)}, bf16[320,1024]{1,0:T(8,128)(2,1)S(1)}, u32[]{:S(2)}, u32[]{:S(2)}) collective-permute-start(bf16[320,1024]{1,0:T(8,128)(2,1)} %own_ref.1), channel_id=1, source_target_pairs={{0,1},{1,0},{2,3},{3,2},{4,5},{5,4},{6,7},{7,6},{8,9},{9,8},{10,11... | collective-permute-start | bytes 1966088 | tf_op jit(solution)/shard_map/ppermute | solution.py:226
  1.6 18.0 %collective-permute-start.3 = (bf16[128,1024]{1,0:T(8,128)(2,1)S(1)}, bf16[128,1024]{1,0:T(8,128)(2,1)S(1)}, u32[]{:S(2)}, u32[]{:S(2)}) collective-permute-start(bf16[128,1024]{1,0:T(8,128)(2,1)S(1)} %get-tuple-element.43), channel_id=1, source_target_pairs={{0,2},{1,3},{2,0},{3,1},{4,6},{5,7},{6,4},{7,5},{8,10},{9,11},{10,... | collective-permute-start | bytes 786440 | tf_op jit(solution)/shard_map/ppermute | solution.py:226
  4.2 15.4 %collective-permute-start = (bf16[192,1024]{1,0:T(8,128)(2,1)S(1)}, bf16[192,1024]{1,0:T(8,128)(2,1)S(1)}, u32[]{:S(2)}, u32[]{:S(2)}) collective-permute-start(bf16[192,1024]{1,0:T(8,128)(2,1)S(1)} %get-tuple-element.28), channel_id=1, source_target_pairs={{0,2},{1,3},{2,0},{3,1},{4,6},{5,7},{6,4},{7,5},{8,10},{9,11},{10,... | collective-permute-start | bytes 1179656 | tf_op jit(solution)/shard_map/ppermute | solution.py:226
  10.3 57.0 %collective-permute-start.22 = (bf16[512,1024]{1,0:T(8,128)(2,1)S(1)}, bf16[512,1024]{1,0:T(8,128)(2,1)S(1)}, u32[]{:S(2)}, u32[]{:S(2)}) collective-permute-start(bf16[512,1024]{1,0:T(8,128)(2,1)S(1)} %get-tuple-element.50), channel_id=1, source_target_pairs={{0,1},{1,0},{2,3},{3,2},{4,5},{5,4},{6,7},{7,6},{8,9},{9,8},{10,11... | collective-permute-start | bytes 3145736 | tf_op jit(solution)/shard_map/ppermute | solution.py:226
  19.6 17.1 %collective-permute-start.1 = (bf16[192,1024]{1,0:T(8,128)(2,1)S(1)}, bf16[192,1024]{1,0:T(8,128)(2,1)S(1)}, u32[]{:S(2)}, u32[]{:S(2)}) collective-permute-start(bf16[192,1024]{1,0:T(8,128)(2,1)S(1)} %collective-permute-done.far_ref), channel_id=1, source_target_pairs={{0,1},{1,0},{2,3},{3,2},{4,5},{5,4},{6,7},{7,6},{8,9},{9,8},{10,11... | collective-permute-start | bytes 1179656 | tf_op jit(solution)/shard_map/ppermute | solution.py:226
  19.6 5.6 %collective-permute-start.4 = (bf16[128,1024]{1,0:T(8,128)(2,1)S(1)}, bf16[128,1024]{1,0:T(8,128)(2,1)S(1)}, u32[]{:S(2)}, u32[]{:S(2)}) collective-permute-start(bf16[128,1024]{1,0:T(8,128)(2,1)S(1)} %collective-permute-done.3.far_ref), channel_id=1, source_target_pairs={{0,1},{1,0},{2,3},{3,2},{4,5},{5,4},{6,7},{7,6},{8,9},{9,8},{10,11... | collective-permute-start | bytes 786440 | tf_op jit(solution)/shard_map/ppermute | solution.py:226
  20.1 3.5 %copy-start = (bf16[320,1024]{1,0:T(8,128)(2,1)S(1)}, bf16[320,1024]{1,0:T(8,128)(2,1)}, u32[]{:S(2)}) copy-start(bf16[320,1024]{1,0:T(8,128)(2,1)} %own_ref.1) | copy-start | bytes 1966084
  20.1 50.4 %collective-permute-start.20 = (bf16[512,1024]{1,0:T(8,128)(2,1)S(1)}, bf16[512,1024]{1,0:T(8,128)(2,1)S(1)}, u32[]{:S(2)}, u32[]{:S(2)}) collective-permute-start(bf16[512,1024]{1,0:T(8,128)(2,1)S(1)} %get-tuple-element.47), channel_id=1, source_target_pairs={{0,1},{1,0},{2,3},{3,2},{4,5},{5,4},{6,7},{7,6},{8,9},{9,8},{10,11... | collective-permute-start | bytes 3145736 | tf_op jit(solution)/shard_map/ppermute | solution.py:226
  25.7 6.7 %collective-permute-start.8 = (bf16[128,256]{1,0:T(8,128)(2,1)S(1)}, bf16[128,256]{1,0:T(8,128)(2,1)S(1)}, u32[]{:S(2)}, u32[]{:S(2)}) collective-permute-start(bf16[128,256]{1,0:T(8,128)(2,1)S(1)} %get-tuple-element.45.refs_4_), channel_id=1, source_target_pairs={{0,8},{4,12},{8,16},{12,20},{16,24},{20,28},{24,0},{28,4},{1,9},{5... | collective-permute-start | bytes 196616 | tf_op jit(solution)/shard_map/ppermute | solution.py:232
  27.5 7.6 %collective-permute-start.12 = (bf16[128,256]{1,0:T(8,128)(2,1)S(1)}, bf16[128,256]{1,0:T(8,128)(2,1)S(1)}, u32[]{:S(2)}, u32[]{:S(2)}) collective-permute-start(bf16[128,256]{1,0:T(8,128)(2,1)S(1)} %get-tuple-element.45.refs_4_), channel_id=1, source_target_pairs={{0,16},{4,20},{8,24},{12,28},{16,0},{20,4},{24,8},{28,12},{1,17},{... | collective-permute-start | bytes 196616 | tf_op jit(solution)/shard_map/ppermute | solution.py:232
  32.4 5.9 %collective-permute-start.16 = (bf16[128,256]{1,0:T(8,128)(2,1)S(1)}, bf16[128,256]{1,0:T(8,128)(2,1)S(1)}, u32[]{:S(2)}, u32[]{:S(2)}) collective-permute-start(bf16[128,256]{1,0:T(8,128)(2,1)S(1)} %get-tuple-element.45.refs_4_), channel_id=1, source_target_pairs={{0,24},{4,28},{8,0},{12,4},{16,8},{20,12},{24,16},{28,20},{1,25},{... | collective-permute-start | bytes 196616 | tf_op jit(solution)/shard_map/ppermute | solution.py:232
  35.1 4.7 %collective-permute-start.6 = (bf16[128,256]{1,0:T(8,128)(2,1)S(1)}, bf16[128,256]{1,0:T(8,128)(2,1)S(1)}, u32[]{:S(2)}, u32[]{:S(2)}) collective-permute-start(bf16[128,256]{1,0:T(8,128)(2,1)S(1)} %get-tuple-element.45.refs_4_), channel_id=1, source_target_pairs={{0,4},{4,0},{8,12},{12,8},{16,20},{20,16},{24,28},{28,24},{1,5},{5... | collective-permute-start | bytes 196616 | tf_op jit(solution)/shard_map/ppermute | solution.py:229
  36.6 4.7 %collective-permute-start.10 = (bf16[128,256]{1,0:T(8,128)(2,1)S(1)}, bf16[128,256]{1,0:T(8,128)(2,1)S(1)}, u32[]{:S(2)}, u32[]{:S(2)}) collective-permute-start(bf16[128,256]{1,0:T(8,128)(2,1)S(1)} %collective-permute-done.8.refs_8_), channel_id=1, source_target_pairs={{0,4},{4,0},{8,12},{12,8},{16,20},{20,16},{24,28},{28,24},{1,5},{5... | collective-permute-start | bytes 196616 | tf_op jit(solution)/shard_map/ppermute | solution.py:229
  38.3 9.0 %collective-permute-start.11 = (bf16[192,256]{1,0:T(8,128)(2,1)S(1)}, bf16[192,256]{1,0:T(8,128)(2,1)S(1)}, u32[]{:S(2)}, u32[]{:S(2)}) collective-permute-start(bf16[192,256]{1,0:T(8,128)(2,1)S(1)} %get-tuple-element.42.refs_3_), channel_id=1, source_target_pairs={{0,16},{4,20},{8,24},{12,28},{16,0},{20,4},{24,8},{28,12},{1,17},{... | collective-permute-start | bytes 294920 | tf_op jit(solution)/shard_map/ppermute | solution.py:232
  39.9 4.3 %collective-permute-start.14 = (bf16[128,256]{1,0:T(8,128)(2,1)S(1)}, bf16[128,256]{1,0:T(8,128)(2,1)S(1)}, u32[]{:S(2)}, u32[]{:S(2)}) collective-permute-start(bf16[128,256]{1,0:T(8,128)(2,1)S(1)} %collective-permute-done.12.refs_12_), channel_id=1, source_target_pairs={{0,4},{4,0},{8,12},{12,8},{16,20},{20,16},{24,28},{28,24},{1,5},{5... | collective-permute-start | bytes 196616 | tf_op jit(solution)/shard_map/ppermute | solution.py:229
  41.3 4.6 %collective-permute-start.18 = (bf16[128,256]{1,0:T(8,128)(2,1)S(1)}, bf16[128,256]{1,0:T(8,128)(2,1)S(1)}, u32[]{:S(2)}, u32[]{:S(2)}) collective-permute-start(bf16[128,256]{1,0:T(8,128)(2,1)S(1)} %collective-permute-done.16.refs_16_), channel_id=1, source_target_pairs={{0,4},{4,0},{8,12},{12,8},{16,20},{20,16},{24,28},{28,24},{1,5},{5... | collective-permute-start | bytes 196616 | tf_op jit(solution)/shard_map/ppermute | solution.py:229
  44.1 5.7 %collective-permute-start.15 = (bf16[192,256]{1,0:T(8,128)(2,1)S(1)}, bf16[192,256]{1,0:T(8,128)(2,1)S(1)}, u32[]{:S(2)}, u32[]{:S(2)}) collective-permute-start(bf16[192,256]{1,0:T(8,128)(2,1)S(1)} %get-tuple-element.42.refs_3_), channel_id=1, source_target_pairs={{0,24},{4,28},{8,0},{12,4},{16,8},{20,12},{24,16},{28,20},{1,25},{... | collective-permute-start | bytes 294920 | tf_op jit(solution)/shard_map/ppermute | solution.py:232
  45.9 6.4 %collective-permute-start.7 = (bf16[192,256]{1,0:T(8,128)(2,1)S(1)}, bf16[192,256]{1,0:T(8,128)(2,1)S(1)}, u32[]{:S(2)}, u32[]{:S(2)}) collective-permute-start(bf16[192,256]{1,0:T(8,128)(2,1)S(1)} %get-tuple-element.42.refs_3_), channel_id=1, source_target_pairs={{0,8},{4,12},{8,16},{12,20},{16,24},{20,28},{24,0},{28,4},{1,9},{5... | collective-permute-start | bytes 294920 | tf_op jit(solution)/shard_map/ppermute | solution.py:232
  47.3 6.0 %collective-permute-start.5 = (bf16[192,256]{1,0:T(8,128)(2,1)S(1)}, bf16[192,256]{1,0:T(8,128)(2,1)S(1)}, u32[]{:S(2)}, u32[]{:S(2)}) collective-permute-start(bf16[192,256]{1,0:T(8,128)(2,1)S(1)} %get-tuple-element.42.refs_3_), channel_id=1, source_target_pairs={{0,4},{4,0},{8,12},{12,8},{16,20},{20,16},{24,28},{28,24},{1,5},{5... | collective-permute-start | bytes 294920 | tf_op jit(solution)/shard_map/ppermute | solution.py:229
  49.8 5.3 %collective-permute-start.13 = (bf16[192,256]{1,0:T(8,128)(2,1)S(1)}, bf16[192,256]{1,0:T(8,128)(2,1)S(1)}, u32[]{:S(2)}, u32[]{:S(2)}) collective-permute-start(bf16[192,256]{1,0:T(8,128)(2,1)S(1)} %collective-permute-done.11.refs_11_), channel_id=1, source_target_pairs={{0,4},{4,0},{8,12},{12,8},{16,20},{20,16},{24,28},{28,24},{1,5},{5... | collective-permute-start | bytes 294920 | tf_op jit(solution)/shard_map/ppermute | solution.py:229
  52.3 4.6 %collective-permute-start.17 = (bf16[192,256]{1,0:T(8,128)(2,1)S(1)}, bf16[192,256]{1,0:T(8,128)(2,1)S(1)}, u32[]{:S(2)}, u32[]{:S(2)}) collective-permute-start(bf16[192,256]{1,0:T(8,128)(2,1)S(1)} %collective-permute-done.15.refs_15_), channel_id=1, source_target_pairs={{0,4},{4,0},{8,12},{12,8},{16,20},{20,16},{24,28},{28,24},{1,5},{5... | collective-permute-start | bytes 294920 | tf_op jit(solution)/shard_map/ppermute | solution.py:229
  53.3 4.7 %collective-permute-start.9 = (bf16[192,256]{1,0:T(8,128)(2,1)S(1)}, bf16[192,256]{1,0:T(8,128)(2,1)S(1)}, u32[]{:S(2)}, u32[]{:S(2)}) collective-permute-start(bf16[192,256]{1,0:T(8,128)(2,1)S(1)} %collective-permute-done.7.refs_7_), channel_id=1, source_target_pairs={{0,4},{4,0},{8,12},{12,8},{16,20},{20,16},{24,28},{28,24},{1,5},{5... | collective-permute-start | bytes 294920 | tf_op jit(solution)/shard_map/ppermute | solution.py:229
  63.0 4.2 %collective-permute-start.19 = (bf16[192,512]{1,0:T(8,128)(2,1)S(1)}, bf16[192,512]{1,0:T(8,128)(2,1)S(1)}, u32[]{:S(2)}, u32[]{:S(2)}) collective-permute-start(bf16[192,512]{1,0:T(8,128)(2,1)S(1)} %shard_map.80.own_ref), channel_id=1, source_target_pairs={{0,1},{1,0},{2,3},{3,2},{4,5},{5,4},{6,7},{7,6},{8,9},{9,8},{10,11... | collective-permute-start | bytes 589832 | tf_op jit(solution)/shard_map/ppermute | solution.py:226
  66.7 2.8 %collective-permute-start.21 = (bf16[128,512]{1,0:T(8,128)(2,1)S(1)}, bf16[128,512]{1,0:T(8,128)(2,1)S(1)}, u32[]{:S(2)}, u32[]{:S(2)}) collective-permute-start(bf16[128,512]{1,0:T(8,128)(2,1)S(1)} %shard_map.83.own_ref), channel_id=1, source_target_pairs={{0,1},{1,0},{2,3},{3,2},{4,5},{5,4},{6,7},{7,6},{8,9},{9,8},{10,11... | collective-permute-start | bytes 393224 | tf_op jit(solution)/shard_map/ppermute | solution.py:226
  67.8 16.7 %collective-permute-start.23 = (bf16[192,1024]{1,0:T(8,128)(2,1)S(1)}, bf16[192,1024]{1,0:T(8,128)(2,1)S(1)}, u32[]{:S(2)}, u32[]{:S(2)}) collective-permute-start(bf16[192,1024]{1,0:T(8,128)(2,1)S(1)} %shard_map.85), channel_id=1, source_target_pairs={{0,2},{1,3},{2,0},{3,1},{4,6},{5,7},{6,4},{7,5},{8,10},{9,11},{10,... | collective-permute-start | bytes 1179656 | tf_op jit(solution)/shard_map/ppermute | solution.py:226
  69.9 14.7 %collective-permute-start.24 = (bf16[128,1024]{1,0:T(8,128)(2,1)S(1)}, bf16[128,1024]{1,0:T(8,128)(2,1)S(1)}, u32[]{:S(2)}, u32[]{:S(2)}) collective-permute-start(bf16[128,1024]{1,0:T(8,128)(2,1)S(1)} %shard_map.86), channel_id=1, source_target_pairs={{0,2},{1,3},{2,0},{3,1},{4,6},{5,7},{6,4},{7,5},{8,10},{9,11},{10,... | collective-permute-start | bytes 786440 | tf_op jit(solution)/shard_map/ppermute | solution.py:226
where the time goes:
time: 85.8 us; the launch traced here: 85.5 us
  waiting for transfers between devices  34.9 us (41%)
  starting transfers between devices  25.1 us (29%)
  Pallas kernels  22.1 us (26%)
  local copies, waits for them, and re-layouts  1.62 us (2%)
  other arithmetic  1.61 us (2%)
    ppermute x11, waiting for transfers between devices, over_col(): return lax.ppermute(value, 'col', [(i, i ^ flip) for i in range(cols)])  22.1 us
    pallas_call x15, Pallas kernels, call(): pl.pallas_call(kernel, out_shape=outs, in_specs=ins, out_specs=jax.tree.m...  22.1 us
    ppermute x6, starting transfers between devices, up(): lax.ppermute(value, 'tok', [(i, (i + 2 * steps) % toks) for i in range(to...  10.3 us
    ppermute x8, starting transfers between devices, across(): return lax.ppermute(value, 'tok', [(i, i ^ 1) for i in range(toks)])  8.08 us
    ppermute x8, waiting for transfers between devices, across(): return lax.ppermute(value, 'tok', [(i, i ^ 1) for i in range(toks)])  7.18 us
    ppermute x11, starting transfers between devices, over_col(): return lax.ppermute(value, 'col', [(i, i ^ flip) for i in range(cols)])  6.79 us
    ppermute x6, waiting for transfers between devices, up(): lax.ppermute(value, 'tok', [(i, (i + 2 * steps) % toks) for i in range(to...  5.67 us
  transfers between devices with their start and end apart: 25, of which 11 were waited for; matrix products, arithmetic and copies ran while one was open for 4% of the time, Pallas kernels for 25%

commit v1 on v0

--- a/solution.py
+++ b/solution.py
@@ -1,4 +1,5 @@
 import functools
+import math
 
 import jax
 import jax.numpy as jnp
@@ -13,6 +14,7 @@
 GROUP_BLOCKS = 4
 ROPE_BASE = 500000.0
 NEG = -1e30
+CODE = 256
 
 
 SMEM = pl.BlockSpec(memory_space=pltpu.SMEM)
@@ -36,7 +38,7 @@
         kernel,
         out_shape=outs,
         in_specs=ins,
-        out_specs=jax.tree.map(lambda _: VMEM, outs),
+        out_specs=jax.tree.map(lambda x: SMEM if x.dtype == jnp.int32 else VMEM, outs),
         scratch_shapes=list(scratch),
         compiler_params=pltpu.CompilerParams(vmem_limit_bytes=vmem << 20),
         cost_estimate=pl.CostEstimate(
@@ -60,13 +62,14 @@
     )
 
 
-def run_copies(pairs, sem):
+def run_copies(pairs, sem, meanwhile=lambda: None):
     copies = [
         pltpu.make_async_copy(source, target, sem.at[index])
         for index, (source, target) in enumerate(pairs)
     ]
     for copy in copies:
         copy.start()
+    meanwhile()
     for copy in copies:
         copy.wait()
 
@@ -90,8 +93,20 @@
     )
 
 
-def rows_kernel(starts_ref, *rest):
-    sources, outs, sem = rest[:3], rest[3:-1], rest[-1]
+def sort_rows(counts_ref, order_ref, heads, qblocks, cuts, groups):
+    for first, last in cuts:
+        at = jnp.int32(first * heads)
+        for wanted in range(groups, 0, -1):
+            for head in range(heads):
+                for block in range(first, last):
+                    live = counts_ref[head * qblocks + block]
+                    order_ref[at] = jnp.int32(head * CODE + block)
+                    needed = (live + GROUP_BLOCKS - 1) // GROUP_BLOCKS
+                    at = at + (needed == wanted).astype(jnp.int32)
+
+
+def rows_kernel(sorting, starts_ref, counts_ref, *rest):
+    sources, outs, order_ref, sem = rest[:3], rest[3:-2], rest[-2], rest[-1]
     feat = outs[0].shape[0]
     pairs = []
     for index, out in enumerate(outs):
@@ -101,7 +116,7 @@
             width = source.shape[1]
             pairs.append((source.at[rows, :], out.at[:, pl.ds(at, width)]))
             at += width
-    run_copies(pairs, sem)
+    run_copies(pairs, sem, lambda: sort_rows(counts_ref, order_ref, *sorting))
 
 
 def near_kernel(spans, own_ref, near_ref, w0, w1, *outs):
@@ -121,6 +136,7 @@
         piece = product[:, at : at + HEAD_SIZE]
         turned = piece * cosine + pltpu.roll(piece, HEAD_SIZE // 2, 1) * sine
         if at < width:
+            turned = turned * (HEAD_SIZE**-0.5 * math.log2(math.e))
             q_ref[:, at : at + HEAD_SIZE] = turned.astype(bf16)
         else:
             kv_ref[:, :HEAD_SIZE] = turned.astype(bf16)
@@ -139,36 +155,47 @@
         out_ref[a:b] = (kept[...] + arrived[...].astype(f32)).astype(bf16)
 
 
-def attend_kernel(heads, qblocks, nsel, count, *refs):
-    offsets_ref, counts_ref, q_ref = refs[:3]
-    parts = refs[3 : 3 + count]
-    out_ref, kv_ref = refs[3 + count :]
-    at = 0
-    for part in parts:
-        kv_ref[at : at + part.shape[0]] = part[...]
-        at += part.shape[0]
+def attend_kernel(heads, place, nsel, spans, fresh, count, *refs):
+    first, last, qblocks = place
+    offsets_ref, counts_ref, order_ref = refs[:3]
+    queries, parts = refs[3 : 3 + len(spans)], refs[3 + len(spans) : 3 + count]
+    if fresh:
+        out_ref, kv_ref, q_ref, o_ref = refs[3 + count :]
+        at = 0
+        for part in parts:
+            kv_ref[at : at + part.shape[0]] = part[...]
+            at += part.shape[0]
+    else:
+        out_ref, q_ref, o_ref = refs[3 + count :]
+        (kv_ref,) = parts
+    for head in range(heads):
+        columns = slice(head * HEAD_SIZE, (head + 1) * HEAD_SIZE)
+        for (a, b), part in zip(spans, queries):
+            q_ref[head, a:b] = part[:, columns]
     width = GROUP_BLOCKS * BLK
-    groups = nsel // GROUP_BLOCKS
-    scale = HEAD_SIZE**-0.5
-
-    def one_qblock(qb, carry):
+
+    def some_rows(start, groups):
         lane = lax.broadcasted_iota(jnp.int32, (BLK, width), 1)
         row = lax.broadcasted_iota(jnp.int32, (BLK, width), 0)
-        rows = pl.ds(pl.multiple_of(qb * BLK, BLK), BLK)
-        for head in range(heads):
-            columns = slice(head * HEAD_SIZE, (head + 1) * HEAD_SIZE)
-            query = q_ref[rows, columns]
-            place = head * qblocks[2] + qblocks[0] + qb
-            live = counts_ref[place]
-            scores = []
-            values = []
+        causal = (lane >= BLK) | (lane <= row)
+        ones = jnp.ones((groups * width, HEAD_SIZE), bf16)
+        places, scores, values = [], [], []
+        for member in range(heads):
+            code = order_ref[start + member]
+            head, block = code // CODE, code % CODE
+            index = head * qblocks + block
+            query = q_ref[head, pl.ds(pl.multiple_of(block * BLK, BLK), BLK)]
+            live = counts_ref[index]
+            places.append((head, block))
+            scores.append([])
+            values.append([])
             for group in range(groups):
                 pieces = []
                 for slot in range(GROUP_BLOCKS):
-                    start = offsets_ref[place * nsel + group * GROUP_BLOCKS + slot]
-                    pieces.append(kv_ref[pl.ds(pl.multiple_of(start, BLK), BLK), :])
+                    at = offsets_ref[index * nsel + group * GROUP_BLOCKS + slot]
+                    pieces.append(kv_ref[pl.ds(pl.multiple_of(at, BLK), BLK), :])
                 both = jnp.concatenate(pieces, axis=0)
-                values.append(both[:, HEAD_SIZE:])
+                values[-1].append(both[:, HEAD_SIZE:])
                 score = lax.dot_general(
                     query,
                     both[:, :HEAD_SIZE],
@@ -177,34 +204,61 @@
                 )
                 allowed = lane < (live - group * GROUP_BLOCKS) * BLK
                 if group == 0:
-                    allowed = allowed & ((lane >= BLK) | (lane <= row))
-                scores.append(jnp.where(allowed, score, NEG))
-            highest = jnp.max(
-                functools.reduce(jnp.maximum, scores), axis=-1, keepdims=True
+                    allowed = allowed & causal
+                scores[-1].append(jnp.where(allowed, score, NEG))
+        highest = [
+            jnp.max(functools.reduce(jnp.maximum, score), axis=-1, keepdims=True)
+            for score in scores
+        ]
+        for (head, block), score, high, value in zip(places, scores, highest, values):
+            weights = jnp.concatenate(
+                [jnp.exp2(piece - high).astype(bf16) for piece in score], axis=1
             )
-            total = jnp.zeros((BLK, width), f32)
-            summed = jnp.zeros((BLK, HEAD_SIZE), f32)
-            for score, value in zip(scores, values):
-                weights = jnp.exp((score - highest) * scale)
-                total = total + weights
-                summed = summed + dot(weights.astype(bf16), value)
-            total = jnp.sum(total, axis=-1, keepdims=True)
-            out_ref[rows, columns] = (summed / total).astype(bf16)
+            both = dot(
+                weights, jnp.concatenate([jnp.concatenate(value, axis=0), ones], axis=1)
+            )
+            target = pl.ds(pl.multiple_of((block - first) * BLK, BLK), BLK)
+            o_ref[head, target] = (both[:, :HEAD_SIZE] / both[:, HEAD_SIZE:]).astype(bf16)
+
+    def one_batch(batch, carry):
+        start = first * heads + batch * heads
+        code = order_ref[start]
+        live = counts_ref[code // CODE * qblocks + code % CODE]
+        needed = (live + GROUP_BLOCKS - 1) // GROUP_BLOCKS
+        for groups in range(1, nsel // GROUP_BLOCKS + 1):
+
+            @pl.when(needed == groups)
+            def _(groups=groups):
+                some_rows(start, groups)
+
         return carry
 
-    lax.fori_loop(0, qblocks[1] - qblocks[0], one_qblock, 0)
-
-
-def attend(offsets, counts, query, parts, heads, qblocks, nsel):
-    pairs = query.size // HEAD_SIZE * nsel * BLK
-    held = sum(part.size for part in parts) * 2 >> 20
+    lax.fori_loop(0, last - first, one_batch, 0)
+    for head in range(heads):
+        out_ref[:, head * HEAD_SIZE : (head + 1) * HEAD_SIZE] = o_ref[head]
+
+
+def attend(lists, queries, parts, place, nsel, spans, fresh):
+    heads = queries[0].shape[1] // HEAD_SIZE
+    first, last, _ = place
+    rows = (last - first) * BLK
+    whole = spans[-1][1]
+    keys = sum(part.shape[0] for part in parts)
+    held = keys * HEAD_SIZE * 4 >> 20
+    out = shape((rows, heads * HEAD_SIZE))
+    pairs = rows * heads * nsel * BLK
     return call(
-        functools.partial(attend_kernel, heads, qblocks, nsel, len(parts)),
-        [SMEM, SMEM, VMEM] + [VMEM] * len(parts),
-        shape(query.shape),
-        (offsets, counts, query, *parts),
+        functools.partial(
+            attend_kernel, heads, place, nsel, spans, fresh, len(queries) + len(parts)
+        ),
+        [SMEM] * len(lists) + [VMEM] * (len(queries) + len(parts)),
+        [out, shape((keys, 2 * HEAD_SIZE))] if fresh else out,
+        (*lists, *queries, *parts),
         4 * pairs * HEAD_SIZE,
-        scratch=[pltpu.VMEM((sum(p.shape[0] for p in parts), 2 * HEAD_SIZE), bf16)],
+        scratch=[
+            pltpu.VMEM((heads, whole, HEAD_SIZE), bf16),
+            pltpu.VMEM((heads, rows, HEAD_SIZE), bf16),
+        ],
         vmem=8 + 3 * held,
         grown=pairs,
     )
@@ -235,6 +289,7 @@
 
     first = (qblocks + 1) // 2 * BLK
     spans = [(0, first), (first, tok_rows)]
+    cuts = [(0, qblocks // 2), (qblocks // 2, qblocks)]
     starts = (col ^ jnp.arange(4, dtype=jnp.int32)) * feat
     pieces = call(
         functools.partial(split_kernel, spans),
@@ -272,11 +327,11 @@
     )
     partner_near = over_col(out_send_near, 1)
     partner_far = over_col(out_send_far, 1)
-    weights = call(
-        rows_kernel,
-        [SMEM, HBM, HBM, HBM],
-        [shape((feat, width))] * 4,
-        (starts, *ws),
+    *weights, order = call(
+        functools.partial(rows_kernel, (heads, qblocks, cuts, nsel // GROUP_BLOCKS)),
+        [SMEM, SMEM, HBM, HBM, HBM],
+        [shape((feat, width))] * 4 + [shape((heads * qblocks + 1,), jnp.int32)],
+        (starts, counts, *ws),
         0,
         scratch=[pltpu.SemaphoreType.DMA((12,))],
     )
@@ -317,9 +372,16 @@
     parts = [piece for shard in shards for piece in shard]
 
     keeps, arrivals = [], []
-    for (a, b), query in zip(spans, queries):
-        rows, qa, qb = b - a, a // BLK, b // BLK
-        attended = attend(offsets, counts, query, parts, heads, (qa, qb, qblocks), nsel)
+    lists = (offsets, counts, order)
+    out_spans = [(first * BLK, last * BLK) for first, last in cuts]
+    for part, (first, last) in enumerate(cuts):
+        rows = (last - first) * BLK
+        attended = attend(
+            lists, queries, parts, (first, last, qblocks), nsel, spans, part == 0
+        )
+        if part == 0:
+            attended, gathered = attended
+            parts = [gathered]
         partner = over_col(attended, 1)
 
         def project(own_w, partner_w, kind):
@@ -335,8 +397,8 @@
         arrivals.append(over_col(sent, 2))
         keeps.append(project(out_own_near, partner_near, f32))
     return call(
-        functools.partial(final_kernel, spans),
-        [VMEM] * (2 * len(spans)),
+        functools.partial(final_kernel, out_spans),
+        [VMEM] * (2 * len(out_spans)),
         shape((tok_rows, feat)),
         (*keeps, *arrivals),
         tok_rows * feat,

time: 85.8 us -> 82.5 us (0.962)
  Pallas kernels: 22.1 us -> 18.2 us
    pallas_call x15, Pallas kernels: 22.1 us -> 18.2 us  [call(): pl.pallas_call(kernel, out_shape=outs, in_specs=ins, out_specs=jax.tree.m...]
    ppermute x11, waiting for transfers between devices: 22.1 us -> 23.1 us  [over_col(): return lax.ppermute(value, 'col', [(i, i ^ flip) for i in range(cols)])]
  transfers between devices with their start and end apart: 25 -> 25, of which waited for: 11 -> 13; matrix products, arithmetic and copies ran while one was open for 4% -> 4% of each run, Pallas kernels for 25% -> 21%
where the time goes in v1:
time: 82.5 us; the launch traced here: 82.3 us
  waiting for transfers between devices  35.6 us (43%)
  starting transfers between devices  25 us (30%)
  Pallas kernels  18.2 us (22%)
  local copies, waits for them, and re-layouts  1.63 us (2%)
  other arithmetic  1.61 us (2%)
    ppermute x11, waiting for transfers between devices, over_col(): return lax.ppermute(value, 'col', [(i, i ^ flip) for i in range(cols)])  23.1 us
    pallas_call x15, Pallas kernels, call(): pl.pallas_call(kernel, out_shape=outs, in_specs=ins, out_specs=jax.tree.m...  18.2 us
    ppermute x6, starting transfers between devices, up(): lax.ppermute(value, 'tok', [(i, (i + 2 * steps) % toks) for i in range(to...  9.62 us
    ppermute x8, starting transfers between devices, across(): return lax.ppermute(value, 'tok', [(i, i ^ 1) for i in range(toks)])  8.72 us
    ppermute x11, starting transfers between devices, over_col(): return lax.ppermute(value, 'col', [(i, i ^ flip) for i in range(cols)])  6.66 us
    ppermute x8, waiting for transfers between devices, across(): return lax.ppermute(value, 'tok', [(i, i ^ 1) for i in range(toks)])  6.65 us
    ppermute x6, waiting for transfers between devices, up(): lax.ppermute(value, 'tok', [(i, (i + 2 * steps) % toks) for i in range(to...  5.87 us
  transfers between devices with their start and end apart: 25, of which 13 were waited for; matrix products, arithmetic and copies ran while one was open for 4% of the time, Pallas kernels for 21%

profile of v1, /device:TPU:0, one launch (start us, length us, event | category | flops | bytes accessed | tf_op | source)
XLA Modules:
  0.0 82.3 jit_solution(9031447966411155459)
XLA Ops:
  0.5 1.1 %shard_map.73 = (bf16[192,1024]{1,0:T(8,128)(2,1)S(1)}, bf16[128,1024]{1,0:T(8,128)(2,1)S(1)}) custom-call(bf16[320,1024]{1,0:T(8,128)(2,1)} %own_ref.1), custom_call_target="tpu_custom_call" | custom-call | bytes 1310720 | tf_op jit(solution)/shard_map/pallas_call | solution.py:37
  1.6 2.6 %collective-permute-start.3 = (bf16[128,1024]{1,0:T(8,128)(2,1)S(1)}, bf16[128,1024]{1,0:T(8,128)(2,1)S(1)}, u32[]{:S(2)}, u32[]{:S(2)}) collective-permute-start(bf16[128,1024]{1,0:T(8,128)(2,1)S(1)} %get-tuple-element.46), channel_id=1, source_target_pairs={{0,2},{1,3},{2,0},{3,1},{4,6},{5,7},{6,4},{7,5},{8,10},{9,11},{10,... | collective-permute-start | bytes 786440 | tf_op jit(solution)/shard_map/ppermute | solution.py:280
  4.3 0.8 copy.9
  6.4 0.8 fusion.6
  7.5 2.8 %shard_map.81 = (bf16[512,1024]{1,0:T(8,128)(2,1)S(1)}, bf16[512,1024]{1,0:T(8,128)(2,1)S(1)}, bf16[512,1024]{1,0:T(8,128)(2,1)S(1)}, bf16[512,1024]{1,0:T(8,128)(2,1)S(1)}) custom-call(s32[4]{0:T(128)S(1)} %xor_multiply_fusion.starts_ref, bf16[512,4096]{1,0:T(8,128)(2,1)} %wo.1), custom_call_target="tpu_custom_call" | custom-call | bytes 8388624 | tf_op jit(solution)/shard_map/pallas_call | solution.py:37
  10.6 9.0 %collective-permute-done.far_ref = bf16[192,1024]{1,0:T(8,128)(2,1)S(1)} collective-permute-done((bf16[192,1024]{1,0:T(8,128)(2,1)S(1)}, bf16[192,1024]{1,0:T(8,128)(2,1)S(1)}, u32[]{:S(2)}, u32[]{:S(2)}) %collective-permute-start) | collective-permute-done | bytes 393248 | tf_op jit(solution)/shard_map/ppermute | solution.py:280
  20.1 4.1 %shard_map.74 = (bf16[1024,768]{1,0:T(8,128)(2,1)S(1)}, bf16[1024,768]{1,0:T(8,128)(2,1)S(1)}, bf16[1024,768]{1,0:T(8,128)(2,1)S(1)}, bf16[1024,768]{1,0:T(8,128)(2,1)S(1)}, s32[21]{0:T(128)S(1)}) custom-call(s32[4]{0:T(128)S(1)} %xor_multiply_fusion.starts_ref, s32[20]{0:T(128)S(1)} %reshape.24.counts_ref.refs_1_, bf16[4096,512]{1,0:T(8,128)(2,1)} %rest_0_.1, ...), custom_call_target="tpu_custom_call" | custom-call | bytes 12583092 | tf_op jit(solution)/shard_map/pallas_call | solution.py:37
  24.2 1.3 %shard_map.75 = (f32[192,768]{1,0:T(8,128)S(1)}, f32[128,768]{1,0:T(8,128)S(1)}) custom-call(bf16[320,1024]{1,0:T(8,128)(2,1)S(1)} %copy-done, bf16[320,1024]{1,0:T(8,128)(2,1)S(1)} %collective-permute-done.2.near_ref, bf16[1024,768]{1,0:T(8,128)(2,1)S(1)} %get-tuple-element.38.w0, bf16[1024,768]{1,0:T(8,128)(2,1)S(1)} %get-tuple-element.39.w1), custom_call_target="tpu_custom_call" | custom-call | flops 1006632960 | bytes 5439488 | tf_op jit(solution)/shard_map/pallas_call | solution.py:37
  26.3 1.8 %collective-permute-start.8 = (bf16[128,256]{1,0:T(8,128)(2,1)S(1)}, bf16[128,256]{1,0:T(8,128)(2,1)S(1)}, u32[]{:S(2)}, u32[]{:S(2)}) collective-permute-start(bf16[128,256]{1,0:T(8,128)(2,1)S(1)} %get-tuple-element.50.refs_6_), channel_id=1, source_target_pairs={{0,8},{4,12},{8,16},{12,20},{16,24},{20,28},{24,0},{28,4},{1,9},{5... | collective-permute-start | bytes 196616 | tf_op jit(solution)/shard_map/ppermute | solution.py:286
  28.2 2.6 %collective-permute-start.12 = (bf16[128,256]{1,0:T(8,128)(2,1)S(1)}, bf16[128,256]{1,0:T(8,128)(2,1)S(1)}, u32[]{:S(2)}, u32[]{:S(2)}) collective-permute-start(bf16[128,256]{1,0:T(8,128)(2,1)S(1)} %get-tuple-element.50.refs_6_), channel_id=1, source_target_pairs={{0,16},{4,20},{8,24},{12,28},{16,0},{20,4},{24,8},{28,12},{1,17},{... | collective-permute-start | bytes 196616 | tf_op jit(solution)/shard_map/ppermute | solution.py:286
  30.8 1.7 %collective-permute-done.8.refs_10_ = bf16[128,256]{1,0:T(8,128)(2,1)S(1)} collective-permute-done((bf16[128,256]{1,0:T(8,128)(2,1)S(1)}, bf16[128,256]{1,0:T(8,128)(2,1)S(1)}, u32[]{:S(2)}, u32[]{:S(2)}) %collective-permute-start.8) | collective-permute-done | bytes 65568 | tf_op jit(solution)/shard_map/ppermute | solution.py:286
  32.5 2.1 %collective-permute-start.16 = (bf16[128,256]{1,0:T(8,128)(2,1)S(1)}, bf16[128,256]{1,0:T(8,128)(2,1)S(1)}, u32[]{:S(2)}, u32[]{:S(2)}) collective-permute-start(bf16[128,256]{1,0:T(8,128)(2,1)S(1)} %get-tuple-element.50.refs_6_), channel_id=1, source_target_pairs={{0,24},{4,28},{8,0},{12,4},{16,8},{20,12},{24,16},{28,20},{1,25},{... | collective-permute-start | bytes 196616 | tf_op jit(solution)/shard_map/ppermute | solution.py:286
  34.6 0.9 %collective-permute-done.12.refs_14_ = bf16[128,256]{1,0:T(8,128)(2,1)S(1)} collective-permute-done((bf16[128,256]{1,0:T(8,128)(2,1)S(1)}, bf16[128,256]{1,0:T(8,128)(2,1)S(1)}, u32[]{:S(2)}, u32[]{:S(2)}) %collective-permute-start.12) | collective-permute-done | bytes 65568 | tf_op jit(solution)/shard_map/ppermute | solution.py:286
  35.5 1.6 %collective-permute-start.6 = (bf16[128,256]{1,0:T(8,128)(2,1)S(1)}, bf16[128,256]{1,0:T(8,128)(2,1)S(1)}, u32[]{:S(2)}, u32[]{:S(2)}) collective-permute-start(bf16[128,256]{1,0:T(8,128)(2,1)S(1)} %get-tuple-element.50.refs_6_), channel_id=1, source_target_pairs={{0,4},{4,0},{8,12},{12,8},{16,20},{20,16},{24,28},{28,24},{1,5},{5... | collective-permute-start | bytes 196616 | tf_op jit(solution)/shard_map/ppermute | solution.py:283
  38.6 0.9 %collective-permute-start.11 = (bf16[192,256]{1,0:T(8,128)(2,1)S(1)}, bf16[192,256]{1,0:T(8,128)(2,1)S(1)}, u32[]{:S(2)}, u32[]{:S(2)}) collective-permute-start(bf16[192,256]{1,0:T(8,128)(2,1)S(1)} %get-tuple-element.49.refs_5_), channel_id=1, source_target_pairs={{0,16},{4,20},{8,24},{12,28},{16,0},{20,4},{24,8},{28,12},{1,17},{... | collective-permute-start | bytes 294920 | tf_op jit(solution)/shard_map/ppermute | solution.py:286
  40.1 1.7 %collective-permute-start.14 = (bf16[128,256]{1,0:T(8,128)(2,1)S(1)}, bf16[128,256]{1,0:T(8,128)(2,1)S(1)}, u32[]{:S(2)}, u32[]{:S(2)}) collective-permute-start(bf16[128,256]{1,0:T(8,128)(2,1)S(1)} %collective-permute-done.12.refs_14_), channel_id=1, source_target_pairs={{0,4},{4,0},{8,12},{12,8},{16,20},{20,16},{24,28},{28,24},{1,5},{5... | collective-permute-start | bytes 196616 | tf_op jit(solution)/shard_map/ppermute | solution.py:283
  42.5 1.9 %collective-permute-done.14.refs_16_ = bf16[128,256]{1,0:T(8,128)(2,1)S(1)} collective-permute-done((bf16[128,256]{1,0:T(8,128)(2,1)S(1)}, bf16[128,256]{1,0:T(8,128)(2,1)S(1)}, u32[]{:S(2)}, u32[]{:S(2)}) %collective-permute-start.14) | collective-permute-done | bytes 65568 | tf_op jit(solution)/shard_map/ppermute | solution.py:283
  44.4 1.4 %collective-permute-start.15 = (bf16[192,256]{1,0:T(8,128)(2,1)S(1)}, bf16[192,256]{1,0:T(8,128)(2,1)S(1)}, u32[]{:S(2)}, u32[]{:S(2)}) collective-permute-start(bf16[192,256]{1,0:T(8,128)(2,1)S(1)} %get-tuple-element.49.refs_5_), channel_id=1, source_target_pairs={{0,24},{4,28},{8,0},{12,4},{16,8},{20,12},{24,16},{28,20},{1,25},{... | collective-permute-start | bytes 294920 | tf_op jit(solution)/shard_map/ppermute | solution.py:286
  46.0 0.9 %collective-permute-start.7 = (bf16[192,256]{1,0:T(8,128)(2,1)S(1)}, bf16[192,256]{1,0:T(8,128)(2,1)S(1)}, u32[]{:S(2)}, u32[]{:S(2)}) collective-permute-start(bf16[192,256]{1,0:T(8,128)(2,1)S(1)} %get-tuple-element.49.refs_5_), channel_id=1, source_target_pairs={{0,8},{4,12},{8,16},{12,20},{16,24},{20,28},{24,0},{28,4},{1,9},{5... | collective-permute-start | bytes 294920 | tf_op jit(solution)/shard_map/ppermute | solution.py:286
  46.9 1.2 %collective-permute-start.5 = (bf16[192,256]{1,0:T(8,128)(2,1)S(1)}, bf16[192,256]{1,0:T(8,128)(2,1)S(1)}, u32[]{:S(2)}, u32[]{:S(2)}) collective-permute-start(bf16[192,256]{1,0:T(8,128)(2,1)S(1)} %get-tuple-element.49.refs_5_), channel_id=1, source_target_pairs={{0,4},{4,0},{8,12},{12,8},{16,20},{20,16},{24,28},{28,24},{1,5},{5... | collective-permute-start | bytes 294920 | tf_op jit(solution)/shard_map/ppermute | solution.py:283
  48.1 2.0 %collective-permute-done.15.refs_17_ = bf16[192,256]{1,0:T(8,128)(2,1)S(1)} collective-permute-done((bf16[192,256]{1,0:T(8,128)(2,1)S(1)}, bf16[192,256]{1,0:T(8,128)(2,1)S(1)}, u32[]{:S(2)}, u32[]{:S(2)}) %collective-permute-start.15) | collective-permute-done | bytes 98336 | tf_op jit(solution)/shard_map/ppermute | solution.py:286
  50.0 1.1 %collective-permute-start.13 = (bf16[192,256]{1,0:T(8,128)(2,1)S(1)}, bf16[192,256]{1,0:T(8,128)(2,1)S(1)}, u32[]{:S(2)}, u32[]{:S(2)}) collective-permute-start(bf16[192,256]{1,0:T(8,128)(2,1)S(1)} %collective-permute-done.11.refs_13_), channel_id=1, source_target_pairs={{0,4},{4,0},{8,12},{12,8},{16,20},{20,16},{24,28},{28,24},{1,5},{5... | collective-permute-start | bytes 294920 | tf_op jit(solution)/shard_map/ppermute | solution.py:283
  51.2 1.3 %collective-permute-done.7.refs_9_ = bf16[192,256]{1,0:T(8,128)(2,1)S(1)} collective-permute-done((bf16[192,256]{1,0:T(8,128)(2,1)S(1)}, bf16[192,256]{1,0:T(8,128)(2,1)S(1)}, u32[]{:S(2)}, u32[]{:S(2)}) %collective-permute-start.7) | collective-permute-done | bytes 98336 | tf_op jit(solution)/shard_map/ppermute | solution.py:286
  52.4 1.3 %collective-permute-start.17 = (bf16[192,256]{1,0:T(8,128)(2,1)S(1)}, bf16[192,256]{1,0:T(8,128)(2,1)S(1)}, u32[]{:S(2)}, u32[]{:S(2)}) collective-permute-start(bf16[192,256]{1,0:T(8,128)(2,1)S(1)} %collective-permute-done.15.refs_17_), channel_id=1, source_target_pairs={{0,4},{4,0},{8,12},{12,8},{16,20},{20,16},{24,28},{28,24},{1,5},{5... | collective-permute-start | bytes 294920 | tf_op jit(solution)/shard_map/ppermute | solution.py:283
  54.8 2.3 %collective-permute-done.17.refs_19_ = bf16[192,256]{1,0:T(8,128)(2,1)S(1)} collective-permute-done((bf16[192,256]{1,0:T(8,128)(2,1)S(1)}, bf16[192,256]{1,0:T(8,128)(2,1)S(1)}, u32[]{:S(2)}, u32[]{:S(2)}) %collective-permute-start.17) | collective-permute-done | bytes 98336 | tf_op jit(solution)/shard_map/ppermute | solution.py:283
  57.1 1.3 %collective-permute-done.9.refs_11_ = bf16[192,256]{1,0:T(8,128)(2,1)S(1)} collective-permute-done((bf16[192,256]{1,0:T(8,128)(2,1)S(1)}, bf16[192,256]{1,0:T(8,128)(2,1)S(1)}, u32[]{:S(2)}, u32[]{:S(2)}) %collective-permute-start.9) | collective-permute-done | bytes 98336 | tf_op jit(solution)/shard_map/ppermute | solution.py:283
  58.3 1.7 %shard_map.80 = (bf16[128,512]{1,0:T(8,128)(2,1)S(1)}, bf16[2560,256]{1,0:T(8,128)(2,1)S(1)}) custom-call(s32[320]{0:T(512)S(1)} %reshape.23.refs_0_, s32[20]{0:T(128)S(1)} %reshape.24.counts_ref.refs_1_, s32[21]{0:T(128)S(1)} %get-tuple-element.37.refs_2_, bf16[192,512]{1,0:T(8,128)(2,1)S(1)} %get-tuple-element.45.refs_3_, ...), custom_call_target="tpu_custom_call" | custom-call | flops 268435456 | bytes 3081636 | tf_op jit(solution)/shard_map/pallas_call | solution.py:37
  60.0 2.3 %shard_map.83.own_ref = bf16[192,512]{1,0:T(8,128)(2,1)S(1)} custom-call(s32[320]{0:T(512)S(1)} %reshape.23.refs_0_, s32[20]{0:T(128)S(1)} %reshape.24.counts_ref.refs_1_, s32[21]{0:T(128)S(1)} %get-tuple-element.37.refs_2_, bf16[192,512]{1,0:T(8,128)(2,1)S(1)} %get-tuple-element.45.refs_3_, bf16[128,512]{1,0:T(8,128)(2,1)S(1)} %get-tuple-element.48.refs_4_, ...), custom_call_target="tpu_custom_call" | custom-call | flops 402653184 | bytes 1836452 | tf_op jit(solution)/shard_map/pallas_call | solution.py:37
  62.9 0.9 %collective-permute-done.21.partner_ref = bf16[192,512]{1,0:T(8,128)(2,1)S(1)} collective-permute-done((bf16[192,512]{1,0:T(8,128)(2,1)S(1)}, bf16[192,512]{1,0:T(8,128)(2,1)S(1)}, u32[]{:S(2)}, u32[]{:S(2)}) %collective-permute-start.21) | collective-permute-done | bytes 196640 | tf_op jit(solution)/shard_map/ppermute | solution.py:280
  64.5 1.6 %collective-permute-start.24 = (bf16[192,1024]{1,0:T(8,128)(2,1)S(1)}, bf16[192,1024]{1,0:T(8,128)(2,1)S(1)}, u32[]{:S(2)}, u32[]{:S(2)}) collective-permute-start(bf16[192,1024]{1,0:T(8,128)(2,1)S(1)} %shard_map.86), channel_id=1, source_target_pairs={{0,2},{1,3},{2,0},{3,1},{4,6},{5,7},{6,4},{7,5},{8,10},{9,11},{10,... | collective-permute-start | bytes 1179656 | tf_op jit(solution)/shard_map/ppermute | solution.py:280
  68.2 13.2 %collective-permute-done.23.refs_2_ = bf16[128,1024]{1,0:T(8,128)(2,1)S(1)} collective-permute-done((bf16[128,1024]{1,0:T(8,128)(2,1)S(1)}, bf16[128,1024]{1,0:T(8,128)(2,1)S(1)}, u32[]{:S(2)}, u32[]{:S(2)}) %collective-permute-start.23) | collective-permute-done | bytes 262176 | tf_op jit(solution)/shard_map/ppermute | solution.py:280
  81.3 0.9 %shard_map.87 = bf16[320,1024]{1,0:T(8,128)(2,1)} custom-call(f32[128,1024]{1,0:T(8,128)S(1)} %shard_map.82.refs_0_, f32[192,1024]{1,0:T(8,128)S(1)} %shard_map.84.refs_1_, bf16[128,1024]{1,0:T(8,128)(2,1)S(1)} %collective-permute-done.23.refs_2_, bf16[192,1024]{1,0:T(8,128)(2,1)S(1)} %collective-permute-done.24.refs_3_), custom_call_target="tpu_custom_call" | custom-call | flops 327680 | bytes 2621440 | tf_op jit(solution)/shard_map/pallas_call | solution.py:37
  (46 shorter events, 11.4 us)
Async XLA Ops:
  0.0 24.2 %collective-permute-start.2 = (bf16[320,1024]{1,0:T(8,128)(2,1)}, bf16[320,1024]{1,0:T(8,128)(2,1)S(1)}, u32[]{:S(2)}, u32[]{:S(2)}) collective-permute-start(bf16[320,1024]{1,0:T(8,128)(2,1)} %own_ref.1), channel_id=1, source_target_pairs={{0,1},{1,0},{2,3},{3,2},{4,5},{5,4},{6,7},{7,6},{8,9},{9,8},{10,11... | collective-permute-start | bytes 1966088 | tf_op jit(solution)/shard_map/ppermute | solution.py:280
  1.6 18.0 %collective-permute-start.3 = (bf16[128,1024]{1,0:T(8,128)(2,1)S(1)}, bf16[128,1024]{1,0:T(8,128)(2,1)S(1)}, u32[]{:S(2)}, u32[]{:S(2)}) collective-permute-start(bf16[128,1024]{1,0:T(8,128)(2,1)S(1)} %get-tuple-element.46), channel_id=1, source_target_pairs={{0,2},{1,3},{2,0},{3,1},{4,6},{5,7},{6,4},{7,5},{8,10},{9,11},{10,... | collective-permute-start | bytes 786440 | tf_op jit(solution)/shard_map/ppermute | solution.py:280
  4.2 15.4 %collective-permute-start = (bf16[192,1024]{1,0:T(8,128)(2,1)S(1)}, bf16[192,1024]{1,0:T(8,128)(2,1)S(1)}, u32[]{:S(2)}, u32[]{:S(2)}) collective-permute-start(bf16[192,1024]{1,0:T(8,128)(2,1)S(1)} %get-tuple-element.31), channel_id=1, source_target_pairs={{0,2},{1,3},{2,0},{3,1},{4,6},{5,7},{6,4},{7,5},{8,10},{9,11},{10,... | collective-permute-start | bytes 1179656 | tf_op jit(solution)/shard_map/ppermute | solution.py:280
  10.3 13.9 %copy-start = (bf16[320,1024]{1,0:T(8,128)(2,1)S(1)}, bf16[320,1024]{1,0:T(8,128)(2,1)}, u32[]{:S(2)}) copy-start(bf16[320,1024]{1,0:T(8,128)(2,1)} %own_ref.1) | copy-start | bytes 1966084
  10.3 52.7 %collective-permute-start.22 = (bf16[512,1024]{1,0:T(8,128)(2,1)S(1)}, bf16[512,1024]{1,0:T(8,128)(2,1)S(1)}, u32[]{:S(2)}, u32[]{:S(2)}) collective-permute-start(bf16[512,1024]{1,0:T(8,128)(2,1)S(1)} %get-tuple-element.56), channel_id=1, source_target_pairs={{0,1},{1,0},{2,3},{3,2},{4,5},{5,4},{6,7},{7,6},{8,9},{9,8},{10,11... | collective-permute-start | bytes 3145736 | tf_op jit(solution)/shard_map/ppermute | solution.py:280
  19.6 17.5 %collective-permute-start.1 = (bf16[192,1024]{1,0:T(8,128)(2,1)S(1)}, bf16[192,1024]{1,0:T(8,128)(2,1)S(1)}, u32[]{:S(2)}, u32[]{:S(2)}) collective-permute-start(bf16[192,1024]{1,0:T(8,128)(2,1)S(1)} %collective-permute-done.far_ref), channel_id=1, source_target_pairs={{0,1},{1,0},{2,3},{3,2},{4,5},{5,4},{6,7},{7,6},{8,9},{9,8},{10,11... | collective-permute-start | bytes 1179656 | tf_op jit(solution)/shard_map/ppermute | solution.py:280
  19.6 6.3 %collective-permute-start.4 = (bf16[128,1024]{1,0:T(8,128)(2,1)S(1)}, bf16[128,1024]{1,0:T(8,128)(2,1)S(1)}, u32[]{:S(2)}, u32[]{:S(2)}) collective-permute-start(bf16[128,1024]{1,0:T(8,128)(2,1)S(1)} %collective-permute-done.3.far_ref), channel_id=1, source_target_pairs={{0,1},{1,0},{2,3},{3,2},{4,5},{5,4},{6,7},{7,6},{8,9},{9,8},{10,11... | collective-permute-start | bytes 786440 | tf_op jit(solution)/shard_map/ppermute | solution.py:280
  26.3 6.2 %collective-permute-start.8 = (bf16[128,256]{1,0:T(8,128)(2,1)S(1)}, bf16[128,256]{1,0:T(8,128)(2,1)S(1)}, u32[]{:S(2)}, u32[]{:S(2)}) collective-permute-start(bf16[128,256]{1,0:T(8,128)(2,1)S(1)} %get-tuple-element.50.refs_6_), channel_id=1, source_target_pairs={{0,8},{4,12},{8,16},{12,20},{16,24},{20,28},{24,0},{28,4},{1,9},{5... | collective-permute-start | bytes 196616 | tf_op jit(solution)/shard_map/ppermute | solution.py:286
  28.2 38.9 %collective-permute-start.20 = (bf16[512,1024]{1,0:T(8,128)(2,1)S(1)}, bf16[512,1024]{1,0:T(8,128)(2,1)S(1)}, u32[]{:S(2)}, u32[]{:S(2)}) collective-permute-start(bf16[512,1024]{1,0:T(8,128)(2,1)S(1)} %get-tuple-element.53), channel_id=1, source_target_pairs={{0,1},{1,0},{2,3},{3,2},{4,5},{5,4},{6,7},{7,6},{8,9},{9,8},{10,11... | collective-permute-start | bytes 3145736 | tf_op jit(solution)/shard_map/ppermute | solution.py:280
  28.2 7.3 %collective-permute-start.12 = (bf16[128,256]{1,0:T(8,128)(2,1)S(1)}, bf16[128,256]{1,0:T(8,128)(2,1)S(1)}, u32[]{:S(2)}, u32[]{:S(2)}) collective-permute-start(bf16[128,256]{1,0:T(8,128)(2,1)S(1)} %get-tuple-element.50.refs_6_), channel_id=1, source_target_pairs={{0,16},{4,20},{8,24},{12,28},{16,0},{20,4},{24,8},{28,12},{1,17},{... | collective-permute-start | bytes 196616 | tf_op jit(solution)/shard_map/ppermute | solution.py:286
  32.5 6.1 %collective-permute-start.16 = (bf16[128,256]{1,0:T(8,128)(2,1)S(1)}, bf16[128,256]{1,0:T(8,128)(2,1)S(1)}, u32[]{:S(2)}, u32[]{:S(2)}) collective-permute-start(bf16[128,256]{1,0:T(8,128)(2,1)S(1)} %get-tuple-element.50.refs_6_), channel_id=1, source_target_pairs={{0,24},{4,28},{8,0},{12,4},{16,8},{20,12},{24,16},{28,20},{1,25},{... | collective-permute-start | bytes 196616 | tf_op jit(solution)/shard_map/ppermute | solution.py:286
  35.5 4.6 %collective-permute-start.6 = (bf16[128,256]{1,0:T(8,128)(2,1)S(1)}, bf16[128,256]{1,0:T(8,128)(2,1)S(1)}, u32[]{:S(2)}, u32[]{:S(2)}) collective-permute-start(bf16[128,256]{1,0:T(8,128)(2,1)S(1)} %get-tuple-element.50.refs_6_), channel_id=1, source_target_pairs={{0,4},{4,0},{8,12},{12,8},{16,20},{20,16},{24,28},{28,24},{1,5},{5... | collective-permute-start | bytes 196616 | tf_op jit(solution)/shard_map/ppermute | solution.py:283
  37.1 4.7 %collective-permute-start.10 = (bf16[128,256]{1,0:T(8,128)(2,1)S(1)}, bf16[128,256]{1,0:T(8,128)(2,1)S(1)}, u32[]{:S(2)}, u32[]{:S(2)}) collective-permute-start(bf16[128,256]{1,0:T(8,128)(2,1)S(1)} %collective-permute-done.8.refs_10_), channel_id=1, source_target_pairs={{0,4},{4,0},{8,12},{12,8},{16,20},{20,16},{24,28},{28,24},{1,5},{5... | collective-permute-start | bytes 196616 | tf_op jit(solution)/shard_map/ppermute | solution.py:283
  38.6 8.3 %collective-permute-start.11 = (bf16[192,256]{1,0:T(8,128)(2,1)S(1)}, bf16[192,256]{1,0:T(8,128)(2,1)S(1)}, u32[]{:S(2)}, u32[]{:S(2)}) collective-permute-start(bf16[192,256]{1,0:T(8,128)(2,1)S(1)} %get-tuple-element.49.refs_5_), channel_id=1, source_target_pairs={{0,16},{4,20},{8,24},{12,28},{16,0},{20,4},{24,8},{28,12},{1,17},{... | collective-permute-start | bytes 294920 | tf_op jit(solution)/shard_map/ppermute | solution.py:286
  40.1 4.3 %collective-permute-start.14 = (bf16[128,256]{1,0:T(8,128)(2,1)S(1)}, bf16[128,256]{1,0:T(8,128)(2,1)S(1)}, u32[]{:S(2)}, u32[]{:S(2)}) collective-permute-start(bf16[128,256]{1,0:T(8,128)(2,1)S(1)} %collective-permute-done.12.refs_14_), channel_id=1, source_target_pairs={{0,4},{4,0},{8,12},{12,8},{16,20},{20,16},{24,28},{28,24},{1,5},{5... | collective-permute-start | bytes 196616 | tf_op jit(solution)/shard_map/ppermute | solution.py:283
  41.8 4.3 %collective-permute-start.18 = (bf16[128,256]{1,0:T(8,128)(2,1)S(1)}, bf16[128,256]{1,0:T(8,128)(2,1)S(1)}, u32[]{:S(2)}, u32[]{:S(2)}) collective-permute-start(bf16[128,256]{1,0:T(8,128)(2,1)S(1)} %collective-permute-done.16.refs_18_), channel_id=1, source_target_pairs={{0,4},{4,0},{8,12},{12,8},{16,20},{20,16},{24,28},{28,24},{1,5},{5... | collective-permute-start | bytes 196616 | tf_op jit(solution)/shard_map/ppermute | solution.py:283
  44.4 5.7 %collective-permute-start.15 = (bf16[192,256]{1,0:T(8,128)(2,1)S(1)}, bf16[192,256]{1,0:T(8,128)(2,1)S(1)}, u32[]{:S(2)}, u32[]{:S(2)}) collective-permute-start(bf16[192,256]{1,0:T(8,128)(2,1)S(1)} %get-tuple-element.49.refs_5_), channel_id=1, source_target_pairs={{0,24},{4,28},{8,0},{12,4},{16,8},{20,12},{24,16},{28,20},{1,25},{... | collective-permute-start | bytes 294920 | tf_op jit(solution)/shard_map/ppermute | solution.py:286
  46.0 6.4 %collective-permute-start.7 = (bf16[192,256]{1,0:T(8,128)(2,1)S(1)}, bf16[192,256]{1,0:T(8,128)(2,1)S(1)}, u32[]{:S(2)}, u32[]{:S(2)}) collective-permute-start(bf16[192,256]{1,0:T(8,128)(2,1)S(1)} %get-tuple-element.49.refs_5_), channel_id=1, source_target_pairs={{0,8},{4,12},{8,16},{12,20},{16,24},{20,28},{24,0},{28,4},{1,9},{5... | collective-permute-start | bytes 294920 | tf_op jit(solution)/shard_map/ppermute | solution.py:286
  46.9 6.8 %collective-permute-start.5 = (bf16[192,256]{1,0:T(8,128)(2,1)S(1)}, bf16[192,256]{1,0:T(8,128)(2,1)S(1)}, u32[]{:S(2)}, u32[]{:S(2)}) collective-permute-start(bf16[192,256]{1,0:T(8,128)(2,1)S(1)} %get-tuple-element.49.refs_5_), channel_id=1, source_target_pairs={{0,4},{4,0},{8,12},{12,8},{16,20},{20,16},{24,28},{28,24},{1,5},{5... | collective-permute-start | bytes 294920 | tf_op jit(solution)/shard_map/ppermute | solution.py:283
  50.0 4.8 %collective-permute-start.13 = (bf16[192,256]{1,0:T(8,128)(2,1)S(1)}, bf16[192,256]{1,0:T(8,128)(2,1)S(1)}, u32[]{:S(2)}, u32[]{:S(2)}) collective-permute-start(bf16[192,256]{1,0:T(8,128)(2,1)S(1)} %collective-permute-done.11.refs_13_), channel_id=1, source_target_pairs={{0,4},{4,0},{8,12},{12,8},{16,20},{20,16},{24,28},{28,24},{1,5},{5... | collective-permute-start | bytes 294920 | tf_op jit(solution)/shard_map/ppermute | solution.py:283
  52.4 4.6 %collective-permute-start.17 = (bf16[192,256]{1,0:T(8,128)(2,1)S(1)}, bf16[192,256]{1,0:T(8,128)(2,1)S(1)}, u32[]{:S(2)}, u32[]{:S(2)}) collective-permute-start(bf16[192,256]{1,0:T(8,128)(2,1)S(1)} %collective-permute-done.15.refs_17_), channel_id=1, source_target_pairs={{0,4},{4,0},{8,12},{12,8},{16,20},{20,16},{24,28},{28,24},{1,5},{5... | collective-permute-start | bytes 294920 | tf_op jit(solution)/shard_map/ppermute | solution.py:283
  53.7 4.6 %collective-permute-start.9 = (bf16[192,256]{1,0:T(8,128)(2,1)S(1)}, bf16[192,256]{1,0:T(8,128)(2,1)S(1)}, u32[]{:S(2)}, u32[]{:S(2)}) collective-permute-start(bf16[192,256]{1,0:T(8,128)(2,1)S(1)} %collective-permute-done.7.refs_9_), channel_id=1, source_target_pairs={{0,4},{4,0},{8,12},{12,8},{16,20},{20,16},{24,28},{28,24},{1,5},{5... | collective-permute-start | bytes 294920 | tf_op jit(solution)/shard_map/ppermute | solution.py:283
  62.4 1.5 %collective-permute-start.21 = (bf16[192,512]{1,0:T(8,128)(2,1)S(1)}, bf16[192,512]{1,0:T(8,128)(2,1)S(1)}, u32[]{:S(2)}, u32[]{:S(2)}) collective-permute-start(bf16[192,512]{1,0:T(8,128)(2,1)S(1)} %shard_map.83.own_ref), channel_id=1, source_target_pairs={{0,1},{1,0},{2,3},{3,2},{4,5},{5,4},{6,7},{7,6},{8,9},{9,8},{10,11... | collective-permute-start | bytes 589832 | tf_op jit(solution)/shard_map/ppermute | solution.py:280
  62.4 3.6 %collective-permute-start.19 = (bf16[128,512]{1,0:T(8,128)(2,1)S(1)}, bf16[128,512]{1,0:T(8,128)(2,1)S(1)}, u32[]{:S(2)}, u32[]{:S(2)}) collective-permute-start(bf16[128,512]{1,0:T(8,128)(2,1)S(1)} %get-tuple-element.51.own_ref), channel_id=1, source_target_pairs={{0,1},{1,0},{2,3},{3,2},{4,5},{5,4},{6,7},{7,6},{8,9},{9,8},{10,11... | collective-permute-start | bytes 393224 | tf_op jit(solution)/shard_map/ppermute | solution.py:280
  64.5 16.8 %collective-permute-start.24 = (bf16[192,1024]{1,0:T(8,128)(2,1)S(1)}, bf16[192,1024]{1,0:T(8,128)(2,1)S(1)}, u32[]{:S(2)}, u32[]{:S(2)}) collective-permute-start(bf16[192,1024]{1,0:T(8,128)(2,1)S(1)} %shard_map.86), channel_id=1, source_target_pairs={{0,2},{1,3},{2,0},{3,1},{4,6},{5,7},{6,4},{7,5},{8,10},{9,11},{10,... | collective-permute-start | bytes 1179656 | tf_op jit(solution)/shard_map/ppermute | solution.py:280
  66.5 14.8 %collective-permute-start.23 = (bf16[128,1024]{1,0:T(8,128)(2,1)S(1)}, bf16[128,1024]{1,0:T(8,128)(2,1)S(1)}, u32[]{:S(2)}, u32[]{:S(2)}) collective-permute-start(bf16[128,1024]{1,0:T(8,128)(2,1)S(1)} %shard_map.85), channel_id=1, source_target_pairs={{0,2},{1,3},{2,0},{3,1},{4,6},{5,7},{6,4},{7,5},{8,10},{9,11},{10,... | collective-permute-start | bytes 786440 | tf_op jit(solution)/shard_map/ppermute | solution.py:280

commit v2 on v1

--- a/solution.py
+++ b/solution.py
@@ -95,14 +95,16 @@
 
 def sort_rows(counts_ref, order_ref, heads, qblocks, cuts, groups):
     for first, last in cuts:
+        members = [(head, block) for head in range(heads) for block in range(first, last)]
+        needed = [
+            (counts_ref[head * qblocks + block] + GROUP_BLOCKS - 1) // GROUP_BLOCKS
+            for head, block in members
+        ]
         at = jnp.int32(first * heads)
         for wanted in range(groups, 0, -1):
-            for head in range(heads):
-                for block in range(first, last):
-                    live = counts_ref[head * qblocks + block]
-                    order_ref[at] = jnp.int32(head * CODE + block)
-                    needed = (live + GROUP_BLOCKS - 1) // GROUP_BLOCKS
-                    at = at + (needed == wanted).astype(jnp.int32)
+            for (head, block), need in zip(members, needed):
+                order_ref[at] = jnp.int32(head * CODE + block)
+                at = at + (need == wanted).astype(jnp.int32)
 
 
 def rows_kernel(sorting, starts_ref, counts_ref, *rest):

time: 82.5 us -> 82.5 us (level)
    ppermute x6, starting transfers between devices: 9.62 us -> 10.7 us  [up(): lax.ppermute(value, 'tok', [(i, (i + 2 * steps) % toks) for i in range(to...]
    ppermute x8, starting transfers between devices: 8.72 us -> 7.7 us  [across(): return lax.ppermute(value, 'tok', [(i, i ^ 1) for i in range(toks)])]
  transfers between devices with their start and end apart: 25 -> 25, of which waited for: 13 -> 12; matrix products, arithmetic and copies ran while one was open for 4% -> 4% of each run, Pallas kernels for 21% -> 21%
where the time goes in v2:
time: 82.5 us; the launch traced here: 82.2 us
  waiting for transfers between devices  35.6 us (43%)
  starting transfers between devices  25.1 us (30%)
  Pallas kernels  18.2 us (22%)
  local copies, waits for them, and re-layouts  1.63 us (2%)
  other arithmetic  1.61 us (2%)
    ppermute x11, waiting for transfers between devices, over_col(): return lax.ppermute(value, 'col', [(i, i ^ flip) for i in range(cols)])  23.1 us
    pallas_call x15, Pallas kernels, call(): pl.pallas_call(kernel, out_shape=outs, in_specs=ins, out_specs=jax.tree.m...  18.2 us
    ppermute x6, starting transfers between devices, up(): lax.ppermute(value, 'tok', [(i, (i + 2 * steps) % toks) for i in range(to...  10.7 us
    ppermute x8, starting transfers between devices, across(): return lax.ppermute(value, 'tok', [(i, i ^ 1) for i in range(toks)])  7.7 us
    ppermute x8, waiting for transfers between devices, across(): return lax.ppermute(value, 'tok', [(i, i ^ 1) for i in range(toks)])  7.38 us
    ppermute x11, starting transfers between devices, over_col(): return lax.ppermute(value, 'col', [(i, i ^ flip) for i in range(cols)])  6.66 us
    ppermute x6, waiting for transfers between devices, up(): lax.ppermute(value, 'tok', [(i, (i + 2 * steps) % toks) for i in range(to...  5.09 us
  transfers between devices with their start and end apart: 25, of which 12 were waited for; matrix products, arithmetic and copies ran while one was open for 4% of the time, Pallas kernels for 21%

profile of v2, /device:TPU:0, one launch (start us, length us, event | category | flops | bytes accessed | tf_op | source)
XLA Modules:
  0.0 82.2 jit_solution(10910663497652479814)
XLA Ops:
  0.5 1.1 %shard_map.73 = (bf16[192,1024]{1,0:T(8,128)(2,1)S(1)}, bf16[128,1024]{1,0:T(8,128)(2,1)S(1)}) custom-call(bf16[320,1024]{1,0:T(8,128)(2,1)} %own_ref.1), custom_call_target="tpu_custom_call" | custom-call | bytes 1310720 | tf_op jit(solution)/shard_map/pallas_call | solution.py:37
  1.6 2.6 %collective-permute-start.3 = (bf16[128,1024]{1,0:T(8,128)(2,1)S(1)}, bf16[128,1024]{1,0:T(8,128)(2,1)S(1)}, u32[]{:S(2)}, u32[]{:S(2)}) collective-permute-start(bf16[128,1024]{1,0:T(8,128)(2,1)S(1)} %get-tuple-element.46), channel_id=1, source_target_pairs={{0,2},{1,3},{2,0},{3,1},{4,6},{5,7},{6,4},{7,5},{8,10},{9,11},{10,... | collective-permute-start | bytes 786440 | tf_op jit(solution)/shard_map/ppermute | solution.py:282
  7.5 2.8 %shard_map.81 = (bf16[512,1024]{1,0:T(8,128)(2,1)S(1)}, bf16[512,1024]{1,0:T(8,128)(2,1)S(1)}, bf16[512,1024]{1,0:T(8,128)(2,1)S(1)}, bf16[512,1024]{1,0:T(8,128)(2,1)S(1)}) custom-call(s32[4]{0:T(128)S(1)} %xor_multiply_fusion.starts_ref, bf16[512,4096]{1,0:T(8,128)(2,1)} %wo.1), custom_call_target="tpu_custom_call" | custom-call | bytes 8388624 | tf_op jit(solution)/shard_map/pallas_call | solution.py:37
  10.6 9.0 %collective-permute-done.far_ref = bf16[192,1024]{1,0:T(8,128)(2,1)S(1)} collective-permute-done((bf16[192,1024]{1,0:T(8,128)(2,1)S(1)}, bf16[192,1024]{1,0:T(8,128)(2,1)S(1)}, u32[]{:S(2)}, u32[]{:S(2)}) %collective-permute-start) | collective-permute-done | bytes 393248 | tf_op jit(solution)/shard_map/ppermute | solution.py:282
  20.1 4.0 %shard_map.74 = (bf16[1024,768]{1,0:T(8,128)(2,1)S(1)}, bf16[1024,768]{1,0:T(8,128)(2,1)S(1)}, bf16[1024,768]{1,0:T(8,128)(2,1)S(1)}, bf16[1024,768]{1,0:T(8,128)(2,1)S(1)}, s32[21]{0:T(128)S(1)}) custom-call(s32[4]{0:T(128)S(1)} %xor_multiply_fusion.starts_ref, s32[20]{0:T(128)S(1)} %reshape.24.counts_ref.refs_1_, bf16[4096,512]{1,0:T(8,128)(2,1)} %rest_0_.1, ...), custom_call_target="tpu_custom_call" | custom-call | bytes 12583092 | tf_op jit(solution)/shard_map/pallas_call | solution.py:37
  24.2 1.2 %shard_map.75 = (f32[192,768]{1,0:T(8,128)S(1)}, f32[128,768]{1,0:T(8,128)S(1)}) custom-call(bf16[320,1024]{1,0:T(8,128)(2,1)S(1)} %copy-done, bf16[320,1024]{1,0:T(8,128)(2,1)S(1)} %collective-permute-done.2.near_ref, bf16[1024,768]{1,0:T(8,128)(2,1)S(1)} %get-tuple-element.38.w0, bf16[1024,768]{1,0:T(8,128)(2,1)S(1)} %get-tuple-element.39.w1), custom_call_target="tpu_custom_call" | custom-call | flops 1006632960 | bytes 5439488 | tf_op jit(solution)/shard_map/pallas_call | solution.py:37
  26.3 1.8 %collective-permute-start.8 = (bf16[128,256]{1,0:T(8,128)(2,1)S(1)}, bf16[128,256]{1,0:T(8,128)(2,1)S(1)}, u32[]{:S(2)}, u32[]{:S(2)}) collective-permute-start(bf16[128,256]{1,0:T(8,128)(2,1)S(1)} %get-tuple-element.50.refs_6_), channel_id=1, source_target_pairs={{0,8},{4,12},{8,16},{12,20},{16,24},{20,28},{24,0},{28,4},{1,9},{5... | collective-permute-start | bytes 196616 | tf_op jit(solution)/shard_map/ppermute | solution.py:288
  28.1 2.6 %collective-permute-start.12 = (bf16[128,256]{1,0:T(8,128)(2,1)S(1)}, bf16[128,256]{1,0:T(8,128)(2,1)S(1)}, u32[]{:S(2)}, u32[]{:S(2)}) collective-permute-start(bf16[128,256]{1,0:T(8,128)(2,1)S(1)} %get-tuple-element.50.refs_6_), channel_id=1, source_target_pairs={{0,16},{4,20},{8,24},{12,28},{16,0},{20,4},{24,8},{28,12},{1,17},{... | collective-permute-start | bytes 196616 | tf_op jit(solution)/shard_map/ppermute | solution.py:288
  30.7 1.7 %collective-permute-done.8.refs_10_ = bf16[128,256]{1,0:T(8,128)(2,1)S(1)} collective-permute-done((bf16[128,256]{1,0:T(8,128)(2,1)S(1)}, bf16[128,256]{1,0:T(8,128)(2,1)S(1)}, u32[]{:S(2)}, u32[]{:S(2)}) %collective-permute-start.8) | collective-permute-done | bytes 65568 | tf_op jit(solution)/shard_map/ppermute | solution.py:288
  32.5 3.3 %collective-permute-start.16 = (bf16[128,256]{1,0:T(8,128)(2,1)S(1)}, bf16[128,256]{1,0:T(8,128)(2,1)S(1)}, u32[]{:S(2)}, u32[]{:S(2)}) collective-permute-start(bf16[128,256]{1,0:T(8,128)(2,1)S(1)} %get-tuple-element.50.refs_6_), channel_id=1, source_target_pairs={{0,24},{4,28},{8,0},{12,4},{16,8},{20,12},{24,16},{28,20},{1,25},{... | collective-permute-start | bytes 196616 | tf_op jit(solution)/shard_map/ppermute | solution.py:288
  35.8 1.2 %collective-permute-start.6 = (bf16[128,256]{1,0:T(8,128)(2,1)S(1)}, bf16[128,256]{1,0:T(8,128)(2,1)S(1)}, u32[]{:S(2)}, u32[]{:S(2)}) collective-permute-start(bf16[128,256]{1,0:T(8,128)(2,1)S(1)} %get-tuple-element.50.refs_6_), channel_id=1, source_target_pairs={{0,4},{4,0},{8,12},{12,8},{16,20},{20,16},{24,28},{28,24},{1,5},{5... | collective-permute-start | bytes 196616 | tf_op jit(solution)/shard_map/ppermute | solution.py:285
  37.0 0.8 collective-permute-start.10
  39.4 1.3 %collective-permute-done.6.refs_8_ = bf16[128,256]{1,0:T(8,128)(2,1)S(1)} collective-permute-done((bf16[128,256]{1,0:T(8,128)(2,1)S(1)}, bf16[128,256]{1,0:T(8,128)(2,1)S(1)}, u32[]{:S(2)}, u32[]{:S(2)}) %collective-permute-start.6) | collective-permute-done | bytes 65568 | tf_op jit(solution)/shard_map/ppermute | solution.py:285
  40.7 1.0 %collective-permute-start.14 = (bf16[128,256]{1,0:T(8,128)(2,1)S(1)}, bf16[128,256]{1,0:T(8,128)(2,1)S(1)}, u32[]{:S(2)}, u32[]{:S(2)}) collective-permute-start(bf16[128,256]{1,0:T(8,128)(2,1)S(1)} %collective-permute-done.12.refs_14_), channel_id=1, source_target_pairs={{0,4},{4,0},{8,12},{12,8},{16,20},{20,16},{24,28},{28,24},{1,5},{5... | collective-permute-start | bytes 196616 | tf_op jit(solution)/shard_map/ppermute | solution.py:285
  41.9 0.9 %collective-permute-start.18 = (bf16[128,256]{1,0:T(8,128)(2,1)S(1)}, bf16[128,256]{1,0:T(8,128)(2,1)S(1)}, u32[]{:S(2)}, u32[]{:S(2)}) collective-permute-start(bf16[128,256]{1,0:T(8,128)(2,1)S(1)} %collective-permute-done.16.refs_18_), channel_id=1, source_target_pairs={{0,4},{4,0},{8,12},{12,8},{16,20},{20,16},{24,28},{28,24},{1,5},{5... | collective-permute-start | bytes 196616 | tf_op jit(solution)/shard_map/ppermute | solution.py:285
  42.8 2.2 %collective-permute-done.14.refs_16_ = bf16[128,256]{1,0:T(8,128)(2,1)S(1)} collective-permute-done((bf16[128,256]{1,0:T(8,128)(2,1)S(1)}, bf16[128,256]{1,0:T(8,128)(2,1)S(1)}, u32[]{:S(2)}, u32[]{:S(2)}) %collective-permute-start.14) | collective-permute-done | bytes 65568 | tf_op jit(solution)/shard_map/ppermute | solution.py:285
  45.0 1.2 %collective-permute-start.15 = (bf16[192,256]{1,0:T(8,128)(2,1)S(1)}, bf16[192,256]{1,0:T(8,128)(2,1)S(1)}, u32[]{:S(2)}, u32[]{:S(2)}) collective-permute-start(bf16[192,256]{1,0:T(8,128)(2,1)S(1)} %get-tuple-element.49.refs_5_), channel_id=1, source_target_pairs={{0,24},{4,28},{8,0},{12,4},{16,8},{20,12},{24,16},{28,20},{1,25},{... | collective-permute-start | bytes 294920 | tf_op jit(solution)/shard_map/ppermute | solution.py:288
  46.2 1.3 %collective-permute-start.7 = (bf16[192,256]{1,0:T(8,128)(2,1)S(1)}, bf16[192,256]{1,0:T(8,128)(2,1)S(1)}, u32[]{:S(2)}, u32[]{:S(2)}) collective-permute-start(bf16[192,256]{1,0:T(8,128)(2,1)S(1)} %get-tuple-element.49.refs_5_), channel_id=1, source_target_pairs={{0,8},{4,12},{8,16},{12,20},{16,24},{20,28},{24,0},{28,4},{1,9},{5... | collective-permute-start | bytes 294920 | tf_op jit(solution)/shard_map/ppermute | solution.py:288
  47.4 1.3 %collective-permute-start.5 = (bf16[192,256]{1,0:T(8,128)(2,1)S(1)}, bf16[192,256]{1,0:T(8,128)(2,1)S(1)}, u32[]{:S(2)}, u32[]{:S(2)}) collective-permute-start(bf16[192,256]{1,0:T(8,128)(2,1)S(1)} %get-tuple-element.49.refs_5_), channel_id=1, source_target_pairs={{0,4},{4,0},{8,12},{12,8},{16,20},{20,16},{24,28},{28,24},{1,5},{5... | collective-permute-start | bytes 294920 | tf_op jit(solution)/shard_map/ppermute | solution.py:285
  48.8 1.9 %collective-permute-done.15.refs_17_ = bf16[192,256]{1,0:T(8,128)(2,1)S(1)} collective-permute-done((bf16[192,256]{1,0:T(8,128)(2,1)S(1)}, bf16[192,256]{1,0:T(8,128)(2,1)S(1)}, u32[]{:S(2)}, u32[]{:S(2)}) %collective-permute-start.15) | collective-permute-done | bytes 98336 | tf_op jit(solution)/shard_map/ppermute | solution.py:288
  51.1 1.4 %collective-permute-done.7.refs_9_ = bf16[192,256]{1,0:T(8,128)(2,1)S(1)} collective-permute-done((bf16[192,256]{1,0:T(8,128)(2,1)S(1)}, bf16[192,256]{1,0:T(8,128)(2,1)S(1)}, u32[]{:S(2)}, u32[]{:S(2)}) %collective-permute-start.7) | collective-permute-done | bytes 98336 | tf_op jit(solution)/shard_map/ppermute | solution.py:288
  52.6 1.1 %collective-permute-start.17 = (bf16[192,256]{1,0:T(8,128)(2,1)S(1)}, bf16[192,256]{1,0:T(8,128)(2,1)S(1)}, u32[]{:S(2)}, u32[]{:S(2)}) collective-permute-start(bf16[192,256]{1,0:T(8,128)(2,1)S(1)} %collective-permute-done.15.refs_17_), channel_id=1, source_target_pairs={{0,4},{4,0},{8,12},{12,8},{16,20},{20,16},{24,28},{28,24},{1,5},{5... | collective-permute-start | bytes 294920 | tf_op jit(solution)/shard_map/ppermute | solution.py:285
  53.7 1.0 %collective-permute-start.9 = (bf16[192,256]{1,0:T(8,128)(2,1)S(1)}, bf16[192,256]{1,0:T(8,128)(2,1)S(1)}, u32[]{:S(2)}, u32[]{:S(2)}) collective-permute-start(bf16[192,256]{1,0:T(8,128)(2,1)S(1)} %collective-permute-done.7.refs_9_), channel_id=1, source_target_pairs={{0,4},{4,0},{8,12},{12,8},{16,20},{20,16},{24,28},{28,24},{1,5},{5... | collective-permute-start | bytes 294920 | tf_op jit(solution)/shard_map/ppermute | solution.py:285
  54.6 1.1 %collective-permute-done.13.refs_15_ = bf16[192,256]{1,0:T(8,128)(2,1)S(1)} collective-permute-done((bf16[192,256]{1,0:T(8,128)(2,1)S(1)}, bf16[192,256]{1,0:T(8,128)(2,1)S(1)}, u32[]{:S(2)}, u32[]{:S(2)}) %collective-permute-start.13) | collective-permute-done | bytes 98336 | tf_op jit(solution)/shard_map/ppermute | solution.py:285
  55.7 1.5 %collective-permute-done.17.refs_19_ = bf16[192,256]{1,0:T(8,128)(2,1)S(1)} collective-permute-done((bf16[192,256]{1,0:T(8,128)(2,1)S(1)}, bf16[192,256]{1,0:T(8,128)(2,1)S(1)}, u32[]{:S(2)}, u32[]{:S(2)}) %collective-permute-start.17) | collective-permute-done | bytes 98336 | tf_op jit(solution)/shard_map/ppermute | solution.py:285
  57.2 1.1 %collective-permute-done.9.refs_11_ = bf16[192,256]{1,0:T(8,128)(2,1)S(1)} collective-permute-done((bf16[192,256]{1,0:T(8,128)(2,1)S(1)}, bf16[192,256]{1,0:T(8,128)(2,1)S(1)}, u32[]{:S(2)}, u32[]{:S(2)}) %collective-permute-start.9) | collective-permute-done | bytes 98336 | tf_op jit(solution)/shard_map/ppermute | solution.py:285
  58.3 1.7 %shard_map.80 = (bf16[128,512]{1,0:T(8,128)(2,1)S(1)}, bf16[2560,256]{1,0:T(8,128)(2,1)S(1)}) custom-call(s32[320]{0:T(512)S(1)} %reshape.23.refs_0_, s32[20]{0:T(128)S(1)} %reshape.24.counts_ref.refs_1_, s32[21]{0:T(128)S(1)} %get-tuple-element.37.refs_2_, bf16[192,512]{1,0:T(8,128)(2,1)S(1)} %get-tuple-element.45.refs_3_, ...), custom_call_target="tpu_custom_call" | custom-call | flops 268435456 | bytes 3081636 | tf_op jit(solution)/shard_map/pallas_call | solution.py:37
  60.0 2.3 %shard_map.83.own_ref = bf16[192,512]{1,0:T(8,128)(2,1)S(1)} custom-call(s32[320]{0:T(512)S(1)} %reshape.23.refs_0_, s32[20]{0:T(128)S(1)} %reshape.24.counts_ref.refs_1_, s32[21]{0:T(128)S(1)} %get-tuple-element.37.refs_2_, bf16[192,512]{1,0:T(8,128)(2,1)S(1)} %get-tuple-element.45.refs_3_, bf16[128,512]{1,0:T(8,128)(2,1)S(1)} %get-tuple-element.48.refs_4_, ...), custom_call_target="tpu_custom_call" | custom-call | flops 402653184 | bytes 1836452 | tf_op jit(solution)/shard_map/pallas_call | solution.py:37
  62.9 0.9 %collective-permute-done.21.partner_ref = bf16[192,512]{1,0:T(8,128)(2,1)S(1)} collective-permute-done((bf16[192,512]{1,0:T(8,128)(2,1)S(1)}, bf16[192,512]{1,0:T(8,128)(2,1)S(1)}, u32[]{:S(2)}, u32[]{:S(2)}) %collective-permute-start.21) | collective-permute-done | bytes 196640 | tf_op jit(solution)/shard_map/ppermute | solution.py:282
  64.4 1.6 %collective-permute-start.24 = (bf16[192,1024]{1,0:T(8,128)(2,1)S(1)}, bf16[192,1024]{1,0:T(8,128)(2,1)S(1)}, u32[]{:S(2)}, u32[]{:S(2)}) collective-permute-start(bf16[192,1024]{1,0:T(8,128)(2,1)S(1)} %shard_map.86), channel_id=1, source_target_pairs={{0,2},{1,3},{2,0},{3,1},{4,6},{5,7},{6,4},{7,5},{8,10},{9,11},{10,... | collective-permute-start | bytes 1179656 | tf_op jit(solution)/shard_map/ppermute | solution.py:282
  68.1 13.1 %collective-permute-done.23.refs_2_ = bf16[128,1024]{1,0:T(8,128)(2,1)S(1)} collective-permute-done((bf16[128,1024]{1,0:T(8,128)(2,1)S(1)}, bf16[128,1024]{1,0:T(8,128)(2,1)S(1)}, u32[]{:S(2)}, u32[]{:S(2)}) %collective-permute-start.23) | collective-permute-done | bytes 262176 | tf_op jit(solution)/shard_map/ppermute | solution.py:282
  81.3 0.9 %shard_map.87 = bf16[320,1024]{1,0:T(8,128)(2,1)} custom-call(f32[128,1024]{1,0:T(8,128)S(1)} %shard_map.82.refs_0_, f32[192,1024]{1,0:T(8,128)S(1)} %shard_map.84.refs_1_, bf16[128,1024]{1,0:T(8,128)(2,1)S(1)} %collective-permute-done.23.refs_2_, bf16[192,1024]{1,0:T(8,128)(2,1)S(1)} %collective-permute-done.24.refs_3_), custom_call_target="tpu_custom_call" | custom-call | flops 327680 | bytes 2621440 | tf_op jit(solution)/shard_map/pallas_call | solution.py:37
  (46 shorter events, 11.0 us)
Async XLA Ops:
  0.0 24.1 %collective-permute-start.2 = (bf16[320,1024]{1,0:T(8,128)(2,1)}, bf16[320,1024]{1,0:T(8,128)(2,1)S(1)}, u32[]{:S(2)}, u32[]{:S(2)}) collective-permute-start(bf16[320,1024]{1,0:T(8,128)(2,1)} %own_ref.1), channel_id=1, source_target_pairs={{0,1},{1,0},{2,3},{3,2},{4,5},{5,4},{6,7},{7,6},{8,9},{9,8},{10,11... | collective-permute-start | bytes 1966088 | tf_op jit(solution)/shard_map/ppermute | solution.py:282
  1.6 18.0 %collective-permute-start.3 = (bf16[128,1024]{1,0:T(8,128)(2,1)S(1)}, bf16[128,1024]{1,0:T(8,128)(2,1)S(1)}, u32[]{:S(2)}, u32[]{:S(2)}) collective-permute-start(bf16[128,1024]{1,0:T(8,128)(2,1)S(1)} %get-tuple-element.46), channel_id=1, source_target_pairs={{0,2},{1,3},{2,0},{3,1},{4,6},{5,7},{6,4},{7,5},{8,10},{9,11},{10,... | collective-permute-start | bytes 786440 | tf_op jit(solution)/shard_map/ppermute | solution.py:282
  4.2 15.4 %collective-permute-start = (bf16[192,1024]{1,0:T(8,128)(2,1)S(1)}, bf16[192,1024]{1,0:T(8,128)(2,1)S(1)}, u32[]{:S(2)}, u32[]{:S(2)}) collective-permute-start(bf16[192,1024]{1,0:T(8,128)(2,1)S(1)} %get-tuple-element.31), channel_id=1, source_target_pairs={{0,2},{1,3},{2,0},{3,1},{4,6},{5,7},{6,4},{7,5},{8,10},{9,11},{10,... | collective-permute-start | bytes 1179656 | tf_op jit(solution)/shard_map/ppermute | solution.py:282
  10.3 13.9 %copy-start = (bf16[320,1024]{1,0:T(8,128)(2,1)S(1)}, bf16[320,1024]{1,0:T(8,128)(2,1)}, u32[]{:S(2)}) copy-start(bf16[320,1024]{1,0:T(8,128)(2,1)} %own_ref.1) | copy-start | bytes 1966084
  10.3 52.6 %collective-permute-start.22 = (bf16[512,1024]{1,0:T(8,128)(2,1)S(1)}, bf16[512,1024]{1,0:T(8,128)(2,1)S(1)}, u32[]{:S(2)}, u32[]{:S(2)}) collective-permute-start(bf16[512,1024]{1,0:T(8,128)(2,1)S(1)} %get-tuple-element.56), channel_id=1, source_target_pairs={{0,1},{1,0},{2,3},{3,2},{4,5},{5,4},{6,7},{7,6},{8,9},{9,8},{10,11... | collective-permute-start | bytes 3145736 | tf_op jit(solution)/shard_map/ppermute | solution.py:282
  19.6 17.5 %collective-permute-start.1 = (bf16[192,1024]{1,0:T(8,128)(2,1)S(1)}, bf16[192,1024]{1,0:T(8,128)(2,1)S(1)}, u32[]{:S(2)}, u32[]{:S(2)}) collective-permute-start(bf16[192,1024]{1,0:T(8,128)(2,1)S(1)} %collective-permute-done.far_ref), channel_id=1, source_target_pairs={{0,1},{1,0},{2,3},{3,2},{4,5},{5,4},{6,7},{7,6},{8,9},{9,8},{10,11... | collective-permute-start | bytes 1179656 | tf_op jit(solution)/shard_map/ppermute | solution.py:282
  19.6 6.2 %collective-permute-start.4 = (bf16[128,1024]{1,0:T(8,128)(2,1)S(1)}, bf16[128,1024]{1,0:T(8,128)(2,1)S(1)}, u32[]{:S(2)}, u32[]{:S(2)}) collective-permute-start(bf16[128,1024]{1,0:T(8,128)(2,1)S(1)} %collective-permute-done.3.far_ref), channel_id=1, source_target_pairs={{0,1},{1,0},{2,3},{3,2},{4,5},{5,4},{6,7},{7,6},{8,9},{9,8},{10,11... | collective-permute-start | bytes 786440 | tf_op jit(solution)/shard_map/ppermute | solution.py:282
  26.3 6.2 %collective-permute-start.8 = (bf16[128,256]{1,0:T(8,128)(2,1)S(1)}, bf16[128,256]{1,0:T(8,128)(2,1)S(1)}, u32[]{:S(2)}, u32[]{:S(2)}) collective-permute-start(bf16[128,256]{1,0:T(8,128)(2,1)S(1)} %get-tuple-element.50.refs_6_), channel_id=1, source_target_pairs={{0,8},{4,12},{8,16},{12,20},{16,24},{20,28},{24,0},{28,4},{1,9},{5... | collective-permute-start | bytes 196616 | tf_op jit(solution)/shard_map/ppermute | solution.py:288
  28.1 38.9 %collective-permute-start.20 = (bf16[512,1024]{1,0:T(8,128)(2,1)S(1)}, bf16[512,1024]{1,0:T(8,128)(2,1)S(1)}, u32[]{:S(2)}, u32[]{:S(2)}) collective-permute-start(bf16[512,1024]{1,0:T(8,128)(2,1)S(1)} %get-tuple-element.53), channel_id=1, source_target_pairs={{0,1},{1,0},{2,3},{3,2},{4,5},{5,4},{6,7},{7,6},{8,9},{9,8},{10,11... | collective-permute-start | bytes 3145736 | tf_op jit(solution)/shard_map/ppermute | solution.py:282
  28.1 7.7 %collective-permute-start.12 = (bf16[128,256]{1,0:T(8,128)(2,1)S(1)}, bf16[128,256]{1,0:T(8,128)(2,1)S(1)}, u32[]{:S(2)}, u32[]{:S(2)}) collective-permute-start(bf16[128,256]{1,0:T(8,128)(2,1)S(1)} %get-tuple-element.50.refs_6_), channel_id=1, source_target_pairs={{0,16},{4,20},{8,24},{12,28},{16,0},{20,4},{24,8},{28,12},{1,17},{... | collective-permute-start | bytes 196616 | tf_op jit(solution)/shard_map/ppermute | solution.py:288
  32.5 6.5 %collective-permute-start.16 = (bf16[128,256]{1,0:T(8,128)(2,1)S(1)}, bf16[128,256]{1,0:T(8,128)(2,1)S(1)}, u32[]{:S(2)}, u32[]{:S(2)}) collective-permute-start(bf16[128,256]{1,0:T(8,128)(2,1)S(1)} %get-tuple-element.50.refs_6_), channel_id=1, source_target_pairs={{0,24},{4,28},{8,0},{12,4},{16,8},{20,12},{24,16},{28,20},{1,25},{... | collective-permute-start | bytes 196616 | tf_op jit(solution)/shard_map/ppermute | solution.py:288
  35.8 4.9 %collective-permute-start.6 = (bf16[128,256]{1,0:T(8,128)(2,1)S(1)}, bf16[128,256]{1,0:T(8,128)(2,1)S(1)}, u32[]{:S(2)}, u32[]{:S(2)}) collective-permute-start(bf16[128,256]{1,0:T(8,128)(2,1)S(1)} %get-tuple-element.50.refs_6_), channel_id=1, source_target_pairs={{0,4},{4,0},{8,12},{12,8},{16,20},{20,16},{24,28},{28,24},{1,5},{5... | collective-permute-start | bytes 196616 | tf_op jit(solution)/shard_map/ppermute | solution.py:285
  37.0 4.8 %collective-permute-start.10 = (bf16[128,256]{1,0:T(8,128)(2,1)S(1)}, bf16[128,256]{1,0:T(8,128)(2,1)S(1)}, u32[]{:S(2)}, u32[]{:S(2)}) collective-permute-start(bf16[128,256]{1,0:T(8,128)(2,1)S(1)} %collective-permute-done.8.refs_10_), channel_id=1, source_target_pairs={{0,4},{4,0},{8,12},{12,8},{16,20},{20,16},{24,28},{28,24},{1,5},{5... | collective-permute-start | bytes 196616 | tf_op jit(solution)/shard_map/ppermute | solution.py:285
  38.9 8.5 %collective-permute-start.11 = (bf16[192,256]{1,0:T(8,128)(2,1)S(1)}, bf16[192,256]{1,0:T(8,128)(2,1)S(1)}, u32[]{:S(2)}, u32[]{:S(2)}) collective-permute-start(bf16[192,256]{1,0:T(8,128)(2,1)S(1)} %get-tuple-element.49.refs_5_), channel_id=1, source_target_pairs={{0,16},{4,20},{8,24},{12,28},{16,0},{20,4},{24,8},{28,12},{1,17},{... | collective-permute-start | bytes 294920 | tf_op jit(solution)/shard_map/ppermute | solution.py:288
  40.7 4.3 %collective-permute-start.14 = (bf16[128,256]{1,0:T(8,128)(2,1)S(1)}, bf16[128,256]{1,0:T(8,128)(2,1)S(1)}, u32[]{:S(2)}, u32[]{:S(2)}) collective-permute-start(bf16[128,256]{1,0:T(8,128)(2,1)S(1)} %collective-permute-done.12.refs_14_), channel_id=1, source_target_pairs={{0,4},{4,0},{8,12},{12,8},{16,20},{20,16},{24,28},{28,24},{1,5},{5... | collective-permute-start | bytes 196616 | tf_op jit(solution)/shard_map/ppermute | solution.py:285
  41.9 4.3 %collective-permute-start.18 = (bf16[128,256]{1,0:T(8,128)(2,1)S(1)}, bf16[128,256]{1,0:T(8,128)(2,1)S(1)}, u32[]{:S(2)}, u32[]{:S(2)}) collective-permute-start(bf16[128,256]{1,0:T(8,128)(2,1)S(1)} %collective-permute-done.16.refs_18_), channel_id=1, source_target_pairs={{0,4},{4,0},{8,12},{12,8},{16,20},{20,16},{24,28},{28,24},{1,5},{5... | collective-permute-start | bytes 196616 | tf_op jit(solution)/shard_map/ppermute | solution.py:285
  45.0 5.7 %collective-permute-start.15 = (bf16[192,256]{1,0:T(8,128)(2,1)S(1)}, bf16[192,256]{1,0:T(8,128)(2,1)S(1)}, u32[]{:S(2)}, u32[]{:S(2)}) collective-permute-start(bf16[192,256]{1,0:T(8,128)(2,1)S(1)} %get-tuple-element.49.refs_5_), channel_id=1, source_target_pairs={{0,24},{4,28},{8,0},{12,4},{16,8},{20,12},{24,16},{28,20},{1,25},{... | collective-permute-start | bytes 294920 | tf_op jit(solution)/shard_map/ppermute | solution.py:288
  46.2 6.4 %collective-permute-start.7 = (bf16[192,256]{1,0:T(8,128)(2,1)S(1)}, bf16[192,256]{1,0:T(8,128)(2,1)S(1)}, u32[]{:S(2)}, u32[]{:S(2)}) collective-permute-start(bf16[192,256]{1,0:T(8,128)(2,1)S(1)} %get-tuple-element.49.refs_5_), channel_id=1, source_target_pairs={{0,8},{4,12},{8,16},{12,20},{16,24},{20,28},{24,0},{28,4},{1,9},{5... | collective-permute-start | bytes 294920 | tf_op jit(solution)/shard_map/ppermute | solution.py:288
  47.4 6.2 %collective-permute-start.5 = (bf16[192,256]{1,0:T(8,128)(2,1)S(1)}, bf16[192,256]{1,0:T(8,128)(2,1)S(1)}, u32[]{:S(2)}, u32[]{:S(2)}) collective-permute-start(bf16[192,256]{1,0:T(8,128)(2,1)S(1)} %get-tuple-element.49.refs_5_), channel_id=1, source_target_pairs={{0,4},{4,0},{8,12},{12,8},{16,20},{20,16},{24,28},{28,24},{1,5},{5... | collective-permute-start | bytes 294920 | tf_op jit(solution)/shard_map/ppermute | solution.py:285
  50.7 5.0 %collective-permute-start.13 = (bf16[192,256]{1,0:T(8,128)(2,1)S(1)}, bf16[192,256]{1,0:T(8,128)(2,1)S(1)}, u32[]{:S(2)}, u32[]{:S(2)}) collective-permute-start(bf16[192,256]{1,0:T(8,128)(2,1)S(1)} %collective-permute-done.11.refs_13_), channel_id=1, source_target_pairs={{0,4},{4,0},{8,12},{12,8},{16,20},{20,16},{24,28},{28,24},{1,5},{5... | collective-permute-start | bytes 294920 | tf_op jit(solution)/shard_map/ppermute | solution.py:285
  52.6 4.6 %collective-permute-start.17 = (bf16[192,256]{1,0:T(8,128)(2,1)S(1)}, bf16[192,256]{1,0:T(8,128)(2,1)S(1)}, u32[]{:S(2)}, u32[]{:S(2)}) collective-permute-start(bf16[192,256]{1,0:T(8,128)(2,1)S(1)} %collective-permute-done.15.refs_17_), channel_id=1, source_target_pairs={{0,4},{4,0},{8,12},{12,8},{16,20},{20,16},{24,28},{28,24},{1,5},{5... | collective-permute-start | bytes 294920 | tf_op jit(solution)/shard_map/ppermute | solution.py:285
  53.7 4.6 %collective-permute-start.9 = (bf16[192,256]{1,0:T(8,128)(2,1)S(1)}, bf16[192,256]{1,0:T(8,128)(2,1)S(1)}, u32[]{:S(2)}, u32[]{:S(2)}) collective-permute-start(bf16[192,256]{1,0:T(8,128)(2,1)S(1)} %collective-permute-done.7.refs_9_), channel_id=1, source_target_pairs={{0,4},{4,0},{8,12},{12,8},{16,20},{20,16},{24,28},{28,24},{1,5},{5... | collective-permute-start | bytes 294920 | tf_op jit(solution)/shard_map/ppermute | solution.py:285
  62.3 1.5 %collective-permute-start.21 = (bf16[192,512]{1,0:T(8,128)(2,1)S(1)}, bf16[192,512]{1,0:T(8,128)(2,1)S(1)}, u32[]{:S(2)}, u32[]{:S(2)}) collective-permute-start(bf16[192,512]{1,0:T(8,128)(2,1)S(1)} %shard_map.83.own_ref), channel_id=1, source_target_pairs={{0,1},{1,0},{2,3},{3,2},{4,5},{5,4},{6,7},{7,6},{8,9},{9,8},{10,11... | collective-permute-start | bytes 589832 | tf_op jit(solution)/shard_map/ppermute | solution.py:282
  62.4 3.6 %collective-permute-start.19 = (bf16[128,512]{1,0:T(8,128)(2,1)S(1)}, bf16[128,512]{1,0:T(8,128)(2,1)S(1)}, u32[]{:S(2)}, u32[]{:S(2)}) collective-permute-start(bf16[128,512]{1,0:T(8,128)(2,1)S(1)} %get-tuple-element.51.own_ref), channel_id=1, source_target_pairs={{0,1},{1,0},{2,3},{3,2},{4,5},{5,4},{6,7},{7,6},{8,9},{9,8},{10,11... | collective-permute-start | bytes 393224 | tf_op jit(solution)/shard_map/ppermute | solution.py:282
  64.4 16.8 %collective-permute-start.24 = (bf16[192,1024]{1,0:T(8,128)(2,1)S(1)}, bf16[192,1024]{1,0:T(8,128)(2,1)S(1)}, u32[]{:S(2)}, u32[]{:S(2)}) collective-permute-start(bf16[192,1024]{1,0:T(8,128)(2,1)S(1)} %shard_map.86), channel_id=1, source_target_pairs={{0,2},{1,3},{2,0},{3,1},{4,6},{5,7},{6,4},{7,5},{8,10},{9,11},{10,... | collective-permute-start | bytes 1179656 | tf_op jit(solution)/shard_map/ppermute | solution.py:282
  66.5 14.8 %collective-permute-start.23 = (bf16[128,1024]{1,0:T(8,128)(2,1)S(1)}, bf16[128,1024]{1,0:T(8,128)(2,1)S(1)}, u32[]{:S(2)}, u32[]{:S(2)}) collective-permute-start(bf16[128,1024]{1,0:T(8,128)(2,1)S(1)} %shard_map.85), channel_id=1, source_target_pairs={{0,2},{1,3},{2,0},{3,1},{4,6},{5,7},{6,4},{7,5},{8,10},{9,11},{10,... | collective-permute-start | bytes 786440 | tf_op jit(solution)/shard_map/ppermute | solution.py:282

commit v3 on v2

--- a/solution.py
+++ b/solution.py
@@ -28,7 +28,7 @@
     return jax.ShapeDtypeStruct(dims, kind)
 
 
-def call(kernel, ins, outs, args, flops, scratch=(), vmem=10, grown=0):
+def call(kernel, ins, outs, args, flops, scratch=(), vmem=10, grown=0, out_spec=VMEM, aliases=()):
     args = [
         pltpu.with_memory_space_constraint(arg, pltpu.HBM) if spec is HBM else arg
         for spec, arg in zip(ins, args)
@@ -38,7 +38,8 @@
         kernel,
         out_shape=outs,
         in_specs=ins,
-        out_specs=jax.tree.map(lambda x: SMEM if x.dtype == jnp.int32 else VMEM, outs),
+        out_specs=jax.tree.map(lambda x: SMEM if x.dtype == jnp.int32 else out_spec, outs),
+        input_output_aliases=dict(aliases),
         scratch_shapes=list(scratch),
         compiler_params=pltpu.CompilerParams(vmem_limit_bytes=vmem << 20),
         cost_estimate=pl.CostEstimate(
@@ -150,11 +151,20 @@
     out_ref[...] = total.astype(out_ref.dtype)
 
 
-def final_kernel(spans, *refs):
-    out_ref = refs[-1]
-    count = len(spans)
-    for (a, b), kept, arrived in zip(spans, refs[:count], refs[count : 2 * count]):
-        out_ref[a:b] = (kept[...] + arrived[...].astype(f32)).astype(bf16)
+def final_kernel(a, kept, arrived, *rest):
+    out_ref, held, sem = rest[-3:]
+    half = held.shape[0] // 2
+    copies = []
+    for index in range(2):
+        at = slice(index * half, (index + 1) * half)
+        held[at] = (kept[at] + arrived[at].astype(f32)).astype(bf16)
+        copy = pltpu.make_async_copy(
+            held.at[at], out_ref.at[pl.ds(a + index * half, half)], sem.at[index]
+        )
+        copy.start()
+        copies.append(copy)
+    for copy in copies:
+        copy.wait()
 
 
 def attend_kernel(heads, place, nsel, spans, fresh, count, *refs):
@@ -293,14 +303,16 @@
     spans = [(0, first), (first, tok_rows)]
     cuts = [(0, qblocks // 2), (qblocks // 2, qblocks)]
     starts = (col ^ jnp.arange(4, dtype=jnp.int32)) * feat
-    pieces = call(
-        functools.partial(split_kernel, spans),
-        [HBM],
-        [shape((b - a, feat)) for a, b in spans],
-        (tokens,),
-        0,
-        scratch=[pltpu.SemaphoreType.DMA((len(spans),))],
-    )
+    pieces = []
+    for span in spans:
+        pieces += call(
+            functools.partial(split_kernel, [span]),
+            [HBM],
+            [shape((span[1] - span[0], feat))],
+            (tokens,),
+            0,
+            scratch=[pltpu.SemaphoreType.DMA((1,))],
+        )
     far_parts = []
     for piece in pieces:
         far_parts.append(over_col(piece, 2))
@@ -398,13 +410,20 @@
         sent = project(out_own_far, partner_far, bf16)
         arrivals.append(over_col(sent, 2))
         keeps.append(project(out_own_near, partner_near, f32))
-    return call(
-        functools.partial(final_kernel, out_spans),
-        [VMEM] * (2 * len(out_spans)),
-        shape((tok_rows, feat)),
-        (*keeps, *arrivals),
-        tok_rows * feat,
-    )
+    out = ()
+    for part, ((a, b), kept, arrived) in enumerate(zip(out_spans, keeps, arrivals)):
+        out = call(
+            functools.partial(final_kernel, a),
+            [VMEM, VMEM, HBM][: 3 if part else 2],
+            shape((tok_rows, feat)),
+            (kept, arrived, *out),
+            (b - a) * feat,
+            scratch=[pltpu.VMEM((b - a, feat), bf16), pltpu.SemaphoreType.DMA((2,))],
+            out_spec=HBM,
+            aliases={2: 0} if part else {},
+        )
+        out = (out,)
+    return out[0]
 
 
 def solution(mesh):

time: 82.5 us -> 82.9 us (level)
  Pallas kernels: 18.2 us -> 19.6 us
  local copies, waits for them, and re-layouts: 1.63 us -> 0.28 us
  waiting for transfers between devices: 35.6 us -> 36.5 us
    pallas_call x15 -> x17, Pallas kernels: 18.2 us -> 19.6 us  [call(): pl.pallas_call(kernel, out_shape=outs, in_specs=ins, out_specs=jax.tree.m...]
    ppermute x11, waiting for transfers between devices: 23.1 us -> 24.1 us  [over_col(): return lax.ppermute(value, 'col', [(i, i ^ flip) for i in range(cols)])]
  transfers between devices with their start and end apart: 25 -> 25, of which waited for: 12 -> 12; matrix products, arithmetic and copies ran while one was open for 4% -> 1% of each run, Pallas kernels for 21% -> 23%
where the time goes in v3:
time: 82.9 us; the launch traced here: 82.7 us
  waiting for transfers between devices  36.5 us (44%)
  starting transfers between devices  25.1 us (30%)
  Pallas kernels  19.6 us (24%)
  other arithmetic  0.91 us (1%)
    ppermute x11, waiting for transfers between devices, over_col(): return lax.ppermute(value, 'col', [(i, i ^ flip) for i in range(cols)])  24.1 us
    pallas_call x17, Pallas kernels, call(): pl.pallas_call(kernel, out_shape=outs, in_specs=ins, out_specs=jax.tree.m...  19.6 us
    ppermute x6, starting transfers between devices, up(): lax.ppermute(value, 'tok', [(i, (i + 2 * steps) % toks) for i in range(to...  10.7 us
    ppermute x8, starting transfers between devices, across(): return lax.ppermute(value, 'tok', [(i, i ^ 1) for i in range(toks)])  7.7 us
    ppermute x8, waiting for transfers between devices, across(): return lax.ppermute(value, 'tok', [(i, i ^ 1) for i in range(toks)])  7.34 us
    ppermute x11, starting transfers between devices, over_col(): return lax.ppermute(value, 'col', [(i, i ^ flip) for i in range(cols)])  6.68 us
    ppermute x6, waiting for transfers between devices, up(): lax.ppermute(value, 'tok', [(i, (i + 2 * steps) % toks) for i in range(to...  5.07 us
  transfers between devices with their start and end apart: 25, of which 12 were waited for; matrix products, arithmetic and copies ran while one was open for 1% of the time, Pallas kernels for 23%

profile of v3, /device:TPU:0, one launch (start us, length us, event | category | flops | bytes accessed | tf_op | source)
XLA Modules:
  0.0 82.7 jit_solution(15430222822963550003)
XLA Ops:
  0.5 1.0 %shard_map.78 = bf16[128,1024]{1,0:T(8,128)(2,1)S(1)} custom-call(bf16[320,1024]{1,0:T(8,128)(2,1)} %tokens.3), custom_call_target="tpu_custom_call" | custom-call | bytes 917504 | tf_op jit(solution)/shard_map/pallas_call | solution.py:37
  1.5 2.6 %collective-permute-start.3 = (bf16[128,1024]{1,0:T(8,128)(2,1)S(1)}, bf16[128,1024]{1,0:T(8,128)(2,1)S(1)}, u32[]{:S(2)}, u32[]{:S(2)}) collective-permute-start(bf16[128,1024]{1,0:T(8,128)(2,1)S(1)} %shard_map.78), channel_id=1, source_target_pairs={{0,2},{1,3},{2,0},{3,1},{4,6},{5,7},{6,4},{7,5},{8,10},{9,11},{10,... | collective-permute-start | bytes 786440 | tf_op jit(solution)/shard_map/ppermute | solution.py:292
  4.1 1.0 %shard_map.73 = bf16[192,1024]{1,0:T(8,128)(2,1)S(1)} custom-call(bf16[320,1024]{1,0:T(8,128)(2,1)} %tokens.3), custom_call_target="tpu_custom_call" | custom-call | bytes 1048576 | tf_op jit(solution)/shard_map/pallas_call | solution.py:37
  6.4 2.8 %shard_map.83 = (bf16[512,1024]{1,0:T(8,128)(2,1)S(1)}, bf16[512,1024]{1,0:T(8,128)(2,1)S(1)}, bf16[512,1024]{1,0:T(8,128)(2,1)S(1)}, bf16[512,1024]{1,0:T(8,128)(2,1)S(1)}) custom-call(s32[4]{0:T(128)S(1)} %xor_multiply_fusion.starts_ref, bf16[512,4096]{1,0:T(8,128)(2,1)} %wo.1), custom_call_target="tpu_custom_call" | custom-call | bytes 8388624 | tf_op jit(solution)/shard_map/pallas_call | solution.py:37
  9.4 10.0 %collective-permute-done.far_ref = bf16[192,1024]{1,0:T(8,128)(2,1)S(1)} collective-permute-done((bf16[192,1024]{1,0:T(8,128)(2,1)S(1)}, bf16[192,1024]{1,0:T(8,128)(2,1)S(1)}, u32[]{:S(2)}, u32[]{:S(2)}) %collective-permute-start) | collective-permute-done | bytes 393248 | tf_op jit(solution)/shard_map/ppermute | solution.py:292
  20.0 4.0 %shard_map.74 = (bf16[1024,768]{1,0:T(8,128)(2,1)S(1)}, bf16[1024,768]{1,0:T(8,128)(2,1)S(1)}, bf16[1024,768]{1,0:T(8,128)(2,1)S(1)}, bf16[1024,768]{1,0:T(8,128)(2,1)S(1)}, s32[21]{0:T(128)S(1)}) custom-call(s32[4]{0:T(128)S(1)} %xor_multiply_fusion.starts_ref, s32[20]{0:T(128)S(1)} %reshape.24.counts_ref.refs_1_, bf16[4096,512]{1,0:T(8,128)(2,1)} %rest_0_.1, ...), custom_call_target="tpu_custom_call" | custom-call | bytes 12583092 | tf_op jit(solution)/shard_map/pallas_call | solution.py:37
  24.0 1.3 %shard_map.75 = (f32[192,768]{1,0:T(8,128)S(1)}, f32[128,768]{1,0:T(8,128)S(1)}) custom-call(bf16[320,1024]{1,0:T(8,128)(2,1)S(1)} %copy-done, bf16[320,1024]{1,0:T(8,128)(2,1)S(1)} %collective-permute-done.2.near_ref, bf16[1024,768]{1,0:T(8,128)(2,1)S(1)} %get-tuple-element.35.w0, bf16[1024,768]{1,0:T(8,128)(2,1)S(1)} %get-tuple-element.36.w1), custom_call_target="tpu_custom_call" | custom-call | flops 1006632960 | bytes 5439488 | tf_op jit(solution)/shard_map/pallas_call | solution.py:37
  26.2 1.8 %collective-permute-start.8 = (bf16[128,256]{1,0:T(8,128)(2,1)S(1)}, bf16[128,256]{1,0:T(8,128)(2,1)S(1)}, u32[]{:S(2)}, u32[]{:S(2)}) collective-permute-start(bf16[128,256]{1,0:T(8,128)(2,1)S(1)} %get-tuple-element.46.refs_6_), channel_id=1, source_target_pairs={{0,8},{4,12},{8,16},{12,20},{16,24},{20,28},{24,0},{28,4},{1,9},{5... | collective-permute-start | bytes 196616 | tf_op jit(solution)/shard_map/ppermute | solution.py:298
  28.0 2.6 %collective-permute-start.12 = (bf16[128,256]{1,0:T(8,128)(2,1)S(1)}, bf16[128,256]{1,0:T(8,128)(2,1)S(1)}, u32[]{:S(2)}, u32[]{:S(2)}) collective-permute-start(bf16[128,256]{1,0:T(8,128)(2,1)S(1)} %get-tuple-element.46.refs_6_), channel_id=1, source_target_pairs={{0,16},{4,20},{8,24},{12,28},{16,0},{20,4},{24,8},{28,12},{1,17},{... | collective-permute-start | bytes 196616 | tf_op jit(solution)/shard_map/ppermute | solution.py:298
  30.6 1.7 %collective-permute-done.8.refs_10_ = bf16[128,256]{1,0:T(8,128)(2,1)S(1)} collective-permute-done((bf16[128,256]{1,0:T(8,128)(2,1)S(1)}, bf16[128,256]{1,0:T(8,128)(2,1)S(1)}, u32[]{:S(2)}, u32[]{:S(2)}) %collective-permute-start.8) | collective-permute-done | bytes 65568 | tf_op jit(solution)/shard_map/ppermute | solution.py:298
  32.3 3.4 %collective-permute-start.16 = (bf16[128,256]{1,0:T(8,128)(2,1)S(1)}, bf16[128,256]{1,0:T(8,128)(2,1)S(1)}, u32[]{:S(2)}, u32[]{:S(2)}) collective-permute-start(bf16[128,256]{1,0:T(8,128)(2,1)S(1)} %get-tuple-element.46.refs_6_), channel_id=1, source_target_pairs={{0,24},{4,28},{8,0},{12,4},{16,8},{20,12},{24,16},{28,20},{1,25},{... | collective-permute-start | bytes 196616 | tf_op jit(solution)/shard_map/ppermute | solution.py:298
  35.7 1.2 %collective-permute-start.6 = (bf16[128,256]{1,0:T(8,128)(2,1)S(1)}, bf16[128,256]{1,0:T(8,128)(2,1)S(1)}, u32[]{:S(2)}, u32[]{:S(2)}) collective-permute-start(bf16[128,256]{1,0:T(8,128)(2,1)S(1)} %get-tuple-element.46.refs_6_), channel_id=1, source_target_pairs={{0,4},{4,0},{8,12},{12,8},{16,20},{20,16},{24,28},{28,24},{1,5},{5... | collective-permute-start | bytes 196616 | tf_op jit(solution)/shard_map/ppermute | solution.py:295
  36.9 0.8 collective-permute-start.10
  39.3 1.3 %collective-permute-done.6.refs_8_ = bf16[128,256]{1,0:T(8,128)(2,1)S(1)} collective-permute-done((bf16[128,256]{1,0:T(8,128)(2,1)S(1)}, bf16[128,256]{1,0:T(8,128)(2,1)S(1)}, u32[]{:S(2)}, u32[]{:S(2)}) %collective-permute-start.6) | collective-permute-done | bytes 65568 | tf_op jit(solution)/shard_map/ppermute | solution.py:295
  40.6 1.0 %collective-permute-start.14 = (bf16[128,256]{1,0:T(8,128)(2,1)S(1)}, bf16[128,256]{1,0:T(8,128)(2,1)S(1)}, u32[]{:S(2)}, u32[]{:S(2)}) collective-permute-start(bf16[128,256]{1,0:T(8,128)(2,1)S(1)} %collective-permute-done.12.refs_14_), channel_id=1, source_target_pairs={{0,4},{4,0},{8,12},{12,8},{16,20},{20,16},{24,28},{28,24},{1,5},{5... | collective-permute-start | bytes 196616 | tf_op jit(solution)/shard_map/ppermute | solution.py:295
  41.8 0.9 %collective-permute-start.18 = (bf16[128,256]{1,0:T(8,128)(2,1)S(1)}, bf16[128,256]{1,0:T(8,128)(2,1)S(1)}, u32[]{:S(2)}, u32[]{:S(2)}) collective-permute-start(bf16[128,256]{1,0:T(8,128)(2,1)S(1)} %collective-permute-done.16.refs_18_), channel_id=1, source_target_pairs={{0,4},{4,0},{8,12},{12,8},{16,20},{20,16},{24,28},{28,24},{1,5},{5... | collective-permute-start | bytes 196616 | tf_op jit(solution)/shard_map/ppermute | solution.py:295
  42.6 2.2 %collective-permute-done.14.refs_16_ = bf16[128,256]{1,0:T(8,128)(2,1)S(1)} collective-permute-done((bf16[128,256]{1,0:T(8,128)(2,1)S(1)}, bf16[128,256]{1,0:T(8,128)(2,1)S(1)}, u32[]{:S(2)}, u32[]{:S(2)}) %collective-permute-start.14) | collective-permute-done | bytes 65568 | tf_op jit(solution)/shard_map/ppermute | solution.py:295
  44.9 1.2 %collective-permute-start.15 = (bf16[192,256]{1,0:T(8,128)(2,1)S(1)}, bf16[192,256]{1,0:T(8,128)(2,1)S(1)}, u32[]{:S(2)}, u32[]{:S(2)}) collective-permute-start(bf16[192,256]{1,0:T(8,128)(2,1)S(1)} %get-tuple-element.45.refs_5_), channel_id=1, source_target_pairs={{0,24},{4,28},{8,0},{12,4},{16,8},{20,12},{24,16},{28,20},{1,25},{... | collective-permute-start | bytes 294920 | tf_op jit(solution)/shard_map/ppermute | solution.py:298
  46.0 1.3 %collective-permute-start.7 = (bf16[192,256]{1,0:T(8,128)(2,1)S(1)}, bf16[192,256]{1,0:T(8,128)(2,1)S(1)}, u32[]{:S(2)}, u32[]{:S(2)}) collective-permute-start(bf16[192,256]{1,0:T(8,128)(2,1)S(1)} %get-tuple-element.45.refs_5_), channel_id=1, source_target_pairs={{0,8},{4,12},{8,16},{12,20},{16,24},{20,28},{24,0},{28,4},{1,9},{5... | collective-permute-start | bytes 294920 | tf_op jit(solution)/shard_map/ppermute | solution.py:298
  47.3 1.3 %collective-permute-start.5 = (bf16[192,256]{1,0:T(8,128)(2,1)S(1)}, bf16[192,256]{1,0:T(8,128)(2,1)S(1)}, u32[]{:S(2)}, u32[]{:S(2)}) collective-permute-start(bf16[192,256]{1,0:T(8,128)(2,1)S(1)} %get-tuple-element.45.refs_5_), channel_id=1, source_target_pairs={{0,4},{4,0},{8,12},{12,8},{16,20},{20,16},{24,28},{28,24},{1,5},{5... | collective-permute-start | bytes 294920 | tf_op jit(solution)/shard_map/ppermute | solution.py:295
  48.6 1.9 %collective-permute-done.15.refs_17_ = bf16[192,256]{1,0:T(8,128)(2,1)S(1)} collective-permute-done((bf16[192,256]{1,0:T(8,128)(2,1)S(1)}, bf16[192,256]{1,0:T(8,128)(2,1)S(1)}, u32[]{:S(2)}, u32[]{:S(2)}) %collective-permute-start.15) | collective-permute-done | bytes 98336 | tf_op jit(solution)/shard_map/ppermute | solution.py:298
  51.0 1.5 %collective-permute-done.7.refs_9_ = bf16[192,256]{1,0:T(8,128)(2,1)S(1)} collective-permute-done((bf16[192,256]{1,0:T(8,128)(2,1)S(1)}, bf16[192,256]{1,0:T(8,128)(2,1)S(1)}, u32[]{:S(2)}, u32[]{:S(2)}) %collective-permute-start.7) | collective-permute-done | bytes 98336 | tf_op jit(solution)/shard_map/ppermute | solution.py:298
  52.5 1.1 %collective-permute-start.17 = (bf16[192,256]{1,0:T(8,128)(2,1)S(1)}, bf16[192,256]{1,0:T(8,128)(2,1)S(1)}, u32[]{:S(2)}, u32[]{:S(2)}) collective-permute-start(bf16[192,256]{1,0:T(8,128)(2,1)S(1)} %collective-permute-done.15.refs_17_), channel_id=1, source_target_pairs={{0,4},{4,0},{8,12},{12,8},{16,20},{20,16},{24,28},{28,24},{1,5},{5... | collective-permute-start | bytes 294920 | tf_op jit(solution)/shard_map/ppermute | solution.py:295
  53.5 1.0 %collective-permute-start.9 = (bf16[192,256]{1,0:T(8,128)(2,1)S(1)}, bf16[192,256]{1,0:T(8,128)(2,1)S(1)}, u32[]{:S(2)}, u32[]{:S(2)}) collective-permute-start(bf16[192,256]{1,0:T(8,128)(2,1)S(1)} %collective-permute-done.7.refs_9_), channel_id=1, source_target_pairs={{0,4},{4,0},{8,12},{12,8},{16,20},{20,16},{24,28},{28,24},{1,5},{5... | collective-permute-start | bytes 294920 | tf_op jit(solution)/shard_map/ppermute | solution.py:295
  54.5 1.0 %collective-permute-done.13.refs_15_ = bf16[192,256]{1,0:T(8,128)(2,1)S(1)} collective-permute-done((bf16[192,256]{1,0:T(8,128)(2,1)S(1)}, bf16[192,256]{1,0:T(8,128)(2,1)S(1)}, u32[]{:S(2)}, u32[]{:S(2)}) %collective-permute-start.13) | collective-permute-done | bytes 98336 | tf_op jit(solution)/shard_map/ppermute | solution.py:295
  55.5 1.6 %collective-permute-done.17.refs_19_ = bf16[192,256]{1,0:T(8,128)(2,1)S(1)} collective-permute-done((bf16[192,256]{1,0:T(8,128)(2,1)S(1)}, bf16[192,256]{1,0:T(8,128)(2,1)S(1)}, u32[]{:S(2)}, u32[]{:S(2)}) %collective-permute-start.17) | collective-permute-done | bytes 98336 | tf_op jit(solution)/shard_map/ppermute | solution.py:295
  57.1 1.1 %collective-permute-done.9.refs_11_ = bf16[192,256]{1,0:T(8,128)(2,1)S(1)} collective-permute-done((bf16[192,256]{1,0:T(8,128)(2,1)S(1)}, bf16[192,256]{1,0:T(8,128)(2,1)S(1)}, u32[]{:S(2)}, u32[]{:S(2)}) %collective-permute-start.9) | collective-permute-done | bytes 98336 | tf_op jit(solution)/shard_map/ppermute | solution.py:295
  58.1 1.7 %shard_map.81 = (bf16[128,512]{1,0:T(8,128)(2,1)S(1)}, bf16[2560,256]{1,0:T(8,128)(2,1)S(1)}) custom-call(s32[320]{0:T(512)S(1)} %reshape.23.refs_0_, s32[20]{0:T(128)S(1)} %reshape.24.counts_ref.refs_1_, s32[21]{0:T(128)S(1)} %get-tuple-element.34.refs_2_, bf16[192,512]{1,0:T(8,128)(2,1)S(1)} %get-tuple-element.42.refs_3_, ...), custom_call_target="tpu_custom_call" | custom-call | flops 268435456 | bytes 3081636 | tf_op jit(solution)/shard_map/pallas_call | solution.py:37
  59.9 2.3 %shard_map.82.own_ref = bf16[192,512]{1,0:T(8,128)(2,1)S(1)} custom-call(s32[320]{0:T(512)S(1)} %reshape.23.refs_0_, s32[20]{0:T(128)S(1)} %reshape.24.counts_ref.refs_1_, s32[21]{0:T(128)S(1)} %get-tuple-element.34.refs_2_, bf16[192,512]{1,0:T(8,128)(2,1)S(1)} %get-tuple-element.42.refs_3_, bf16[128,512]{1,0:T(8,128)(2,1)S(1)} %get-tuple-element.44.refs_4_, ...), custom_call_target="tpu_custom_call" | custom-call | flops 402653184 | bytes 1836452 | tf_op jit(solution)/shard_map/pallas_call | solution.py:37
  62.8 0.9 %collective-permute-done.19.partner_ref = bf16[192,512]{1,0:T(8,128)(2,1)S(1)} collective-permute-done((bf16[192,512]{1,0:T(8,128)(2,1)S(1)}, bf16[192,512]{1,0:T(8,128)(2,1)S(1)}, u32[]{:S(2)}, u32[]{:S(2)}) %collective-permute-start.19) | collective-permute-done | bytes 196640 | tf_op jit(solution)/shard_map/ppermute | solution.py:292
  64.3 1.6 %collective-permute-start.22 = (bf16[192,1024]{1,0:T(8,128)(2,1)S(1)}, bf16[192,1024]{1,0:T(8,128)(2,1)S(1)}, u32[]{:S(2)}, u32[]{:S(2)}) collective-permute-start(bf16[192,1024]{1,0:T(8,128)(2,1)S(1)} %shard_map.85), channel_id=1, source_target_pairs={{0,2},{1,3},{2,0},{3,1},{4,6},{5,7},{6,4},{7,5},{8,10},{9,11},{10,... | collective-permute-start | bytes 1179656 | tf_op jit(solution)/shard_map/ppermute | solution.py:292
  68.0 13.1 %collective-permute-done.24.arrived = bf16[128,1024]{1,0:T(8,128)(2,1)S(1)} collective-permute-done((bf16[128,1024]{1,0:T(8,128)(2,1)S(1)}, bf16[128,1024]{1,0:T(8,128)(2,1)S(1)}, u32[]{:S(2)}, u32[]{:S(2)}) %collective-permute-start.24) | collective-permute-done | bytes 262176 | tf_op jit(solution)/shard_map/ppermute | solution.py:292
  (52 shorter events, 10.5 us)
Async XLA Ops:
  0.0 6.0 %copy-start.1 = (s32[4,5,16]{2,0,1:T(4,128)S(1)}, s32[4,5,16]{2,0,1:T(4,128)}, u32[]{:S(2)}) copy-start(s32[4,5,16]{2,0,1:T(4,128)} %param.12) | copy-start | bytes 3844
  0.0 5.2 %copy-start.2 = (s32[4,5]{1,0:T(4,128)S(1)}, s32[4,5]{1,0:T(4,128)}, u32[]{:S(2)}) copy-start(s32[4,5]{1,0:T(4,128)} %param.13) | copy-start | bytes 244
  0.0 24.0 %collective-permute-start.2 = (bf16[320,1024]{1,0:T(8,128)(2,1)}, bf16[320,1024]{1,0:T(8,128)(2,1)S(1)}, u32[]{:S(2)}, u32[]{:S(2)}) collective-permute-start(bf16[320,1024]{1,0:T(8,128)(2,1)} %tokens.3), channel_id=1, source_target_pairs={{0,1},{1,0},{2,3},{3,2},{4,5},{5,4},{6,7},{7,6},{8,9},{9,8},{10,11... | collective-permute-start | bytes 1966088 | tf_op jit(solution)/shard_map/ppermute | solution.py:292
  1.5 18.0 %collective-permute-start.3 = (bf16[128,1024]{1,0:T(8,128)(2,1)S(1)}, bf16[128,1024]{1,0:T(8,128)(2,1)S(1)}, u32[]{:S(2)}, u32[]{:S(2)}) collective-permute-start(bf16[128,1024]{1,0:T(8,128)(2,1)S(1)} %shard_map.78), channel_id=1, source_target_pairs={{0,2},{1,3},{2,0},{3,1},{4,6},{5,7},{6,4},{7,5},{8,10},{9,11},{10,... | collective-permute-start | bytes 786440 | tf_op jit(solution)/shard_map/ppermute | solution.py:292
  5.1 14.4 %collective-permute-start = (bf16[192,1024]{1,0:T(8,128)(2,1)S(1)}, bf16[192,1024]{1,0:T(8,128)(2,1)S(1)}, u32[]{:S(2)}, u32[]{:S(2)}) collective-permute-start(bf16[192,1024]{1,0:T(8,128)(2,1)S(1)} %shard_map.73), channel_id=1, source_target_pairs={{0,2},{1,3},{2,0},{3,1},{4,6},{5,7},{6,4},{7,5},{8,10},{9,11},{10,... | collective-permute-start | bytes 1179656 | tf_op jit(solution)/shard_map/ppermute | solution.py:292
  9.2 14.9 %copy-start = (bf16[320,1024]{1,0:T(8,128)(2,1)S(1)}, bf16[320,1024]{1,0:T(8,128)(2,1)}, u32[]{:S(2)}) copy-start(bf16[320,1024]{1,0:T(8,128)(2,1)} %tokens.3) | copy-start | bytes 1966084
  9.2 53.6 %collective-permute-start.21 = (bf16[512,1024]{1,0:T(8,128)(2,1)S(1)}, bf16[512,1024]{1,0:T(8,128)(2,1)S(1)}, u32[]{:S(2)}, u32[]{:S(2)}) collective-permute-start(bf16[512,1024]{1,0:T(8,128)(2,1)S(1)} %get-tuple-element.51), channel_id=1, source_target_pairs={{0,1},{1,0},{2,3},{3,2},{4,5},{5,4},{6,7},{7,6},{8,9},{9,8},{10,11... | collective-permute-start | bytes 3145736 | tf_op jit(solution)/shard_map/ppermute | solution.py:292
  19.4 17.5 %collective-permute-start.1 = (bf16[192,1024]{1,0:T(8,128)(2,1)S(1)}, bf16[192,1024]{1,0:T(8,128)(2,1)S(1)}, u32[]{:S(2)}, u32[]{:S(2)}) collective-permute-start(bf16[192,1024]{1,0:T(8,128)(2,1)S(1)} %collective-permute-done.far_ref), channel_id=1, source_target_pairs={{0,1},{1,0},{2,3},{3,2},{4,5},{5,4},{6,7},{7,6},{8,9},{9,8},{10,11... | collective-permute-start | bytes 1179656 | tf_op jit(solution)/shard_map/ppermute | solution.py:292
  19.4 6.2 %collective-permute-start.4 = (bf16[128,1024]{1,0:T(8,128)(2,1)S(1)}, bf16[128,1024]{1,0:T(8,128)(2,1)S(1)}, u32[]{:S(2)}, u32[]{:S(2)}) collective-permute-start(bf16[128,1024]{1,0:T(8,128)(2,1)S(1)} %collective-permute-done.3.far_ref), channel_id=1, source_target_pairs={{0,1},{1,0},{2,3},{3,2},{4,5},{5,4},{6,7},{7,6},{8,9},{9,8},{10,11... | collective-permute-start | bytes 786440 | tf_op jit(solution)/shard_map/ppermute | solution.py:292
  26.2 6.1 %collective-permute-start.8 = (bf16[128,256]{1,0:T(8,128)(2,1)S(1)}, bf16[128,256]{1,0:T(8,128)(2,1)S(1)}, u32[]{:S(2)}, u32[]{:S(2)}) collective-permute-start(bf16[128,256]{1,0:T(8,128)(2,1)S(1)} %get-tuple-element.46.refs_6_), channel_id=1, source_target_pairs={{0,8},{4,12},{8,16},{12,20},{16,24},{20,28},{24,0},{28,4},{1,9},{5... | collective-permute-start | bytes 196616 | tf_op jit(solution)/shard_map/ppermute | solution.py:298
  28.0 38.9 %collective-permute-start.20 = (bf16[512,1024]{1,0:T(8,128)(2,1)S(1)}, bf16[512,1024]{1,0:T(8,128)(2,1)S(1)}, u32[]{:S(2)}, u32[]{:S(2)}) collective-permute-start(bf16[512,1024]{1,0:T(8,128)(2,1)S(1)} %get-tuple-element.49), channel_id=1, source_target_pairs={{0,1},{1,0},{2,3},{3,2},{4,5},{5,4},{6,7},{7,6},{8,9},{9,8},{10,11... | collective-permute-start | bytes 3145736 | tf_op jit(solution)/shard_map/ppermute | solution.py:292
  28.0 7.7 %collective-permute-start.12 = (bf16[128,256]{1,0:T(8,128)(2,1)S(1)}, bf16[128,256]{1,0:T(8,128)(2,1)S(1)}, u32[]{:S(2)}, u32[]{:S(2)}) collective-permute-start(bf16[128,256]{1,0:T(8,128)(2,1)S(1)} %get-tuple-element.46.refs_6_), channel_id=1, source_target_pairs={{0,16},{4,20},{8,24},{12,28},{16,0},{20,4},{24,8},{28,12},{1,17},{... | collective-permute-start | bytes 196616 | tf_op jit(solution)/shard_map/ppermute | solution.py:298
  32.3 6.5 %collective-permute-start.16 = (bf16[128,256]{1,0:T(8,128)(2,1)S(1)}, bf16[128,256]{1,0:T(8,128)(2,1)S(1)}, u32[]{:S(2)}, u32[]{:S(2)}) collective-permute-start(bf16[128,256]{1,0:T(8,128)(2,1)S(1)} %get-tuple-element.46.refs_6_), channel_id=1, source_target_pairs={{0,24},{4,28},{8,0},{12,4},{16,8},{20,12},{24,16},{28,20},{1,25},{... | collective-permute-start | bytes 196616 | tf_op jit(solution)/shard_map/ppermute | solution.py:298
  35.7 4.9 %collective-permute-start.6 = (bf16[128,256]{1,0:T(8,128)(2,1)S(1)}, bf16[128,256]{1,0:T(8,128)(2,1)S(1)}, u32[]{:S(2)}, u32[]{:S(2)}) collective-permute-start(bf16[128,256]{1,0:T(8,128)(2,1)S(1)} %get-tuple-element.46.refs_6_), channel_id=1, source_target_pairs={{0,4},{4,0},{8,12},{12,8},{16,20},{20,16},{24,28},{28,24},{1,5},{5... | collective-permute-start | bytes 196616 | tf_op jit(solution)/shard_map/ppermute | solution.py:295
  36.9 4.8 %collective-permute-start.10 = (bf16[128,256]{1,0:T(8,128)(2,1)S(1)}, bf16[128,256]{1,0:T(8,128)(2,1)S(1)}, u32[]{:S(2)}, u32[]{:S(2)}) collective-permute-start(bf16[128,256]{1,0:T(8,128)(2,1)S(1)} %collective-permute-done.8.refs_10_), channel_id=1, source_target_pairs={{0,4},{4,0},{8,12},{12,8},{16,20},{20,16},{24,28},{28,24},{1,5},{5... | collective-permute-start | bytes 196616 | tf_op jit(solution)/shard_map/ppermute | solution.py:295
  38.8 8.5 %collective-permute-start.11 = (bf16[192,256]{1,0:T(8,128)(2,1)S(1)}, bf16[192,256]{1,0:T(8,128)(2,1)S(1)}, u32[]{:S(2)}, u32[]{:S(2)}) collective-permute-start(bf16[192,256]{1,0:T(8,128)(2,1)S(1)} %get-tuple-element.45.refs_5_), channel_id=1, source_target_pairs={{0,16},{4,20},{8,24},{12,28},{16,0},{20,4},{24,8},{28,12},{1,17},{... | collective-permute-start | bytes 294920 | tf_op jit(solution)/shard_map/ppermute | solution.py:298
  40.6 4.3 %collective-permute-start.14 = (bf16[128,256]{1,0:T(8,128)(2,1)S(1)}, bf16[128,256]{1,0:T(8,128)(2,1)S(1)}, u32[]{:S(2)}, u32[]{:S(2)}) collective-permute-start(bf16[128,256]{1,0:T(8,128)(2,1)S(1)} %collective-permute-done.12.refs_14_), channel_id=1, source_target_pairs={{0,4},{4,0},{8,12},{12,8},{16,20},{20,16},{24,28},{28,24},{1,5},{5... | collective-permute-start | bytes 196616 | tf_op jit(solution)/shard_map/ppermute | solution.py:295
  41.8 4.3 %collective-permute-start.18 = (bf16[128,256]{1,0:T(8,128)(2,1)S(1)}, bf16[128,256]{1,0:T(8,128)(2,1)S(1)}, u32[]{:S(2)}, u32[]{:S(2)}) collective-permute-start(bf16[128,256]{1,0:T(8,128)(2,1)S(1)} %collective-permute-done.16.refs_18_), channel_id=1, source_target_pairs={{0,4},{4,0},{8,12},{12,8},{16,20},{20,16},{24,28},{28,24},{1,5},{5... | collective-permute-start | bytes 196616 | tf_op jit(solution)/shard_map/ppermute | solution.py:295
  44.9 5.7 %collective-permute-start.15 = (bf16[192,256]{1,0:T(8,128)(2,1)S(1)}, bf16[192,256]{1,0:T(8,128)(2,1)S(1)}, u32[]{:S(2)}, u32[]{:S(2)}) collective-permute-start(bf16[192,256]{1,0:T(8,128)(2,1)S(1)} %get-tuple-element.45.refs_5_), channel_id=1, source_target_pairs={{0,24},{4,28},{8,0},{12,4},{16,8},{20,12},{24,16},{28,20},{1,25},{... | collective-permute-start | bytes 294920 | tf_op jit(solution)/shard_map/ppermute | solution.py:298
  46.0 6.4 %collective-permute-start.7 = (bf16[192,256]{1,0:T(8,128)(2,1)S(1)}, bf16[192,256]{1,0:T(8,128)(2,1)S(1)}, u32[]{:S(2)}, u32[]{:S(2)}) collective-permute-start(bf16[192,256]{1,0:T(8,128)(2,1)S(1)} %get-tuple-element.45.refs_5_), channel_id=1, source_target_pairs={{0,8},{4,12},{8,16},{12,20},{16,24},{20,28},{24,0},{28,4},{1,9},{5... | collective-permute-start | bytes 294920 | tf_op jit(solution)/shard_map/ppermute | solution.py:298
  47.3 6.2 %collective-permute-start.5 = (bf16[192,256]{1,0:T(8,128)(2,1)S(1)}, bf16[192,256]{1,0:T(8,128)(2,1)S(1)}, u32[]{:S(2)}, u32[]{:S(2)}) collective-permute-start(bf16[192,256]{1,0:T(8,128)(2,1)S(1)} %get-tuple-element.45.refs_5_), channel_id=1, source_target_pairs={{0,4},{4,0},{8,12},{12,8},{16,20},{20,16},{24,28},{28,24},{1,5},{5... | collective-permute-start | bytes 294920 | tf_op jit(solution)/shard_map/ppermute | solution.py:295
  50.5 5.0 %collective-permute-start.13 = (bf16[192,256]{1,0:T(8,128)(2,1)S(1)}, bf16[192,256]{1,0:T(8,128)(2,1)S(1)}, u32[]{:S(2)}, u32[]{:S(2)}) collective-permute-start(bf16[192,256]{1,0:T(8,128)(2,1)S(1)} %collective-permute-done.11.refs_13_), channel_id=1, source_target_pairs={{0,4},{4,0},{8,12},{12,8},{16,20},{20,16},{24,28},{28,24},{1,5},{5... | collective-permute-start | bytes 294920 | tf_op jit(solution)/shard_map/ppermute | solution.py:295
  52.5 4.6 %collective-permute-start.17 = (bf16[192,256]{1,0:T(8,128)(2,1)S(1)}, bf16[192,256]{1,0:T(8,128)(2,1)S(1)}, u32[]{:S(2)}, u32[]{:S(2)}) collective-permute-start(bf16[192,256]{1,0:T(8,128)(2,1)S(1)} %collective-permute-done.15.refs_17_), channel_id=1, source_target_pairs={{0,4},{4,0},{8,12},{12,8},{16,20},{20,16},{24,28},{28,24},{1,5},{5... | collective-permute-start | bytes 294920 | tf_op jit(solution)/shard_map/ppermute | solution.py:295
  53.5 4.6 %collective-permute-start.9 = (bf16[192,256]{1,0:T(8,128)(2,1)S(1)}, bf16[192,256]{1,0:T(8,128)(2,1)S(1)}, u32[]{:S(2)}, u32[]{:S(2)}) collective-permute-start(bf16[192,256]{1,0:T(8,128)(2,1)S(1)} %collective-permute-done.7.refs_9_), channel_id=1, source_target_pairs={{0,4},{4,0},{8,12},{12,8},{16,20},{20,16},{24,28},{28,24},{1,5},{5... | collective-permute-start | bytes 294920 | tf_op jit(solution)/shard_map/ppermute | solution.py:295
  62.2 1.5 %collective-permute-start.19 = (bf16[192,512]{1,0:T(8,128)(2,1)S(1)}, bf16[192,512]{1,0:T(8,128)(2,1)S(1)}, u32[]{:S(2)}, u32[]{:S(2)}) collective-permute-start(bf16[192,512]{1,0:T(8,128)(2,1)S(1)} %shard_map.82.own_ref), channel_id=1, source_target_pairs={{0,1},{1,0},{2,3},{3,2},{4,5},{5,4},{6,7},{7,6},{8,9},{9,8},{10,11... | collective-permute-start | bytes 589832 | tf_op jit(solution)/shard_map/ppermute | solution.py:292
  62.3 3.6 %collective-permute-start.23 = (bf16[128,512]{1,0:T(8,128)(2,1)S(1)}, bf16[128,512]{1,0:T(8,128)(2,1)S(1)}, u32[]{:S(2)}, u32[]{:S(2)}) collective-permute-start(bf16[128,512]{1,0:T(8,128)(2,1)S(1)} %get-tuple-element.52.own_ref), channel_id=1, source_target_pairs={{0,1},{1,0},{2,3},{3,2},{4,5},{5,4},{6,7},{7,6},{8,9},{9,8},{10,11... | collective-permute-start | bytes 393224 | tf_op jit(solution)/shard_map/ppermute | solution.py:292
  64.3 17.6 %collective-permute-start.22 = (bf16[192,1024]{1,0:T(8,128)(2,1)S(1)}, bf16[192,1024]{1,0:T(8,128)(2,1)S(1)}, u32[]{:S(2)}, u32[]{:S(2)}) collective-permute-start(bf16[192,1024]{1,0:T(8,128)(2,1)S(1)} %shard_map.85), channel_id=1, source_target_pairs={{0,2},{1,3},{2,0},{3,1},{4,6},{5,7},{6,4},{7,5},{8,10},{9,11},{10,... | collective-permute-start | bytes 1179656 | tf_op jit(solution)/shard_map/ppermute | solution.py:292
  66.4 14.8 %collective-permute-start.24 = (bf16[128,1024]{1,0:T(8,128)(2,1)S(1)}, bf16[128,1024]{1,0:T(8,128)(2,1)S(1)}, u32[]{:S(2)}, u32[]{:S(2)}) collective-permute-start(bf16[128,1024]{1,0:T(8,128)(2,1)S(1)} %shard_map.87), channel_id=1, source_target_pairs={{0,2},{1,3},{2,0},{3,1},{4,6},{5,7},{6,4},{7,5},{8,10},{9,11},{10,... | collective-permute-start | bytes 786440 | tf_op jit(solution)/shard_map/ppermute | solution.py:292
